TPU v7x, 256 devices: a whole 4x4x8 slice. The times are simulated.
256 devices in a mesh: lam: 128 (over z, y_hi, x, core), atom: 2 (over y_lo).
Axes of the slice: x: 4, y: 4 (y_hi: 2, y_lo: 2; y = y_hi * 2 + y_lo), z: 8, core: 2. Of those that a mesh axis runs over, the one named last changes fastest.
Arguments:
- coords: float32 [128, 3, 16384], P('lam', None, 'atom'), may hold values from 0 to 1
- velocities: float32 [128, 3, 16384], P('lam', None, 'atom'), may hold values from -6 to 6
- coupling: float32 [128, 2, 16384], P('lam', None, 'atom'), may hold values from 0.2 to 1
- charges: float32 [16384], replicated, may hold values from -1.5 to 1.5
- types: int32 [16384], replicated, may hold values from 0 to 15
- type_sigma: float32 [16], replicated, may hold values from 0.25 to 0.4
- type_eps: float32 [16], replicated, may hold values from 0.1 to 1
- near_tiles: int32 [128, 5], P('atom'), may hold values from 0 to 127
- accept: int32 [128], replicated, may hold values from 0 to 1, as said below
Outputs:
- energies: float32 [128, 3], P('lam')
- forces: float32 [128, 3, 16384], P('lam', None, 'atom')
- new_coords: float32 [128, 3, 16384], P('lam', None, 'atom')
- new_velocities: float32 [128, 3, 16384], P('lam', None, 'atom')
Inputs may be any that keep to these rules, and one draw needn't show every extreme that they name: accept[r] = 1 exchanges replicas r and r + 1 (modulo 128); no two consecutive entries around the cycle are both 1.
All inputs are finite; a program needn't handle non-finite values.
Results may differ from a plain program's by a relative error of at most 0.0003.
Values sent between devices are 32-bit elements; how exact they have to be, the bound alone decides.
No kernel may reach another device: no remote copies, remote signals or barrier semaphores. Data moves between devices by JAX's collectives and lax.ppermute only.
A program may use at most 64 MiB of HBM per device.

v0:
```python
from functools import partial
import math

import jax
import jax.numpy as jnp
from jax import lax
from jax.sharding import PartitionSpec as P

TILE = 128


DELTA_SOFT = 0.05


def sent_together(arrays, axis, dim, along):
    ends, at = ([], 0)
    for a in arrays[:-1]:
        at += a.shape[along]
        ends.append(at)
    both = jnp.concatenate(arrays, axis=along)
    return tuple(jnp.split(lax.all_gather(both, axis, axis=dim, tiled=True), ends, axis=along))


def passed_along(x, axis, by):
    peers = lax.axis_size(axis)
    return lax.ppermute(x, axis, [(i, (i + by) % peers) for i in range(peers)])


def from_everyone(x, axis):
    copies = jnp.broadcast_to(x, (lax.axis_size(axis), *x.shape))
    return lax.all_to_all(copies, axis, split_axis=0, concat_axis=0, tiled=True)


def over_copies(x, axis):
    everything = from_everyone(x, axis)
    return jnp.sum(everything, axis=0)


def packed_total(arrays, axis):
    ends = [0]
    for a in arrays:
        ends.append(ends[-1] + a.size)
    subtotal = over_copies(jnp.concatenate([a.ravel() for a in arrays]), axis)
    return tuple((subtotal[b:e].reshape(a.shape) for a, b, e in zip(arrays, ends, ends[1:])))


def atom_params(charges, types, type_sigma, type_eps, coupling_whole):
    levels = lax.broadcasted_iota(jnp.int32, (type_sigma.shape[0], types.shape[0]), 0)
    onehot = (levels == types[None, :]).astype(jnp.float32)
    table = jnp.stack([type_sigma, jnp.sqrt(type_eps)])
    looked = jnp.dot(table, onehot, precision=lax.Precision.HIGHEST)
    return jnp.stack([charges * coupling_whole[0], looked[1] * coupling_whole[1], looked[0]])


def pair_block(inputs, with_force):
    rows_pos, cols_pos, rows_par, cols_par, rows_idx, cols_idx = inputs
    delta = rows_pos[:, :, None, :, None] - cols_pos[:, :, :, None, :]
    squared = jnp.sum(delta * delta, axis=0)
    charge_pair = rows_par[0][:, None, :, None] * cols_par[0][:, :, None, :]
    depth_pair = rows_par[1][:, None, :, None] * cols_par[1][:, :, None, :]
    sigma_pair = 0.5 * (rows_par[2][:, None, :, None] + cols_par[2][:, :, None, :])
    sigma_area = sigma_pair * sigma_pair
    pair_keep = (rows_idx[:, None, :, None] != cols_idx[:, :, None, :]).astype(jnp.float32)
    inverse = lax.rsqrt(squared + DELTA_SOFT)
    ratio = sigma_area / (squared + sigma_area)
    cubed = ratio * ratio * ratio
    energy_pair = charge_pair * inverse + 4.0 * depth_pair * (cubed * cubed - cubed)
    total = jnp.sum(energy_pair * pair_keep)
    if not with_force:
        return (total, jnp.zeros_like(rows_pos))
    slope = (
        -0.5 * charge_pair * inverse * inverse * inverse
        - 4.0
        * depth_pair
        * (6.0 * cubed * ratio * ratio - 3.0 * ratio * ratio)
        * ratio
        * ratio
        / sigma_area
    )
    weight = -2.0 * slope * pair_keep
    force = jnp.sum(weight[None] * delta, axis=(2, 4))
    return (total, force)


def evaluate(own_rows, whole, params, first_row, tile_list, with_force):
    count = own_rows.shape[1]
    row_tiles = count // TILE
    group = math.gcd(row_tiles, 4)
    blocks = row_tiles // group
    listed = tile_list.shape[1]
    rows_pos = own_rows.reshape(3, blocks, group, TILE).transpose(1, 0, 2, 3)
    own_par = lax.dynamic_slice_in_dim(params, first_row, count, 1)
    rows_par = own_par.reshape(3, blocks, group, TILE).transpose(1, 0, 2, 3)
    cols_pos = (
        whole.reshape(3, -1, TILE)[:, tile_list]
        .reshape(3, blocks, group, listed, TILE)
        .transpose(1, 0, 2, 3, 4)
    )
    cols_par = (
        params.reshape(3, -1, TILE)[:, tile_list]
        .reshape(3, blocks, group, listed, TILE)
        .transpose(1, 0, 2, 3, 4)
    )
    rows_idx = (first_row + jnp.arange(count, dtype=jnp.int32)).reshape(blocks, group, TILE)
    cols_idx = (
        tile_list[:, :, None] * TILE + jnp.arange(TILE, dtype=jnp.int32)[None, None, :]
    ).reshape(blocks, group, listed, TILE)
    totals, forces = lax.map(
        partial(pair_block, with_force=with_force),
        (rows_pos, cols_pos, rows_par, cols_par, rows_idx, cols_idx),
    )
    return (jnp.sum(totals), forces.transpose(1, 0, 2, 3).reshape(3, count))


def per_device(
    coords, velocities, coupling, charges, types, type_sigma, type_eps, near_tiles, accept
):
    own_coords = coords[0]
    moving = velocities[0]
    width = own_coords.shape[1]
    first_row = lax.axis_index("atom") * width
    whole_own, whole_coupling = sent_together((own_coords, coupling[0]), "atom", 1, 0)
    params = atom_params(charges, types, type_sigma, type_eps, whole_coupling)
    lower_coords, lower_moving = passed_along((own_coords, moving), "lam", 1)
    upper_coords, upper_moving = passed_along((own_coords, moving), "lam", -1)
    lower_whole, upper_whole = sent_together((lower_coords, upper_coords), "atom", 1, 0)
    energy_own, force = evaluate(own_coords, whole_own, params, first_row, near_tiles, True)
    energy_low, unused = evaluate(lower_coords, lower_whole, params, first_row, near_tiles, False)
    energy_up, unused = evaluate(upper_coords, upper_whole, params, first_row, near_tiles, False)
    scale = 0.5 / (width * lax.axis_size("atom"))
    energy_own, energy_low, energy_up = packed_total(
        (energy_own * scale, energy_low * scale, energy_up * scale), "atom"
    )
    from_upper = passed_along(energy_low, "lam", -1)
    from_lower = passed_along(energy_up, "lam", 1)
    energies = jnp.stack([energy_own, from_lower, from_upper])[None]
    replica = lax.axis_index("lam")
    cycle_size = lax.axis_size("lam")
    upper_flag = accept[replica] == 1
    lower_flag = accept[(replica + cycle_size - 1) % cycle_size] == 1
    new_coords = jnp.where(
        upper_flag, upper_coords, jnp.where(lower_flag, lower_coords, own_coords)
    )
    new_velocities = jnp.where(
        upper_flag, upper_moving, jnp.where(lower_flag, lower_moving, moving)
    )
    return (energies, force[None], new_coords[None], new_velocities[None])


def solution(mesh):
    in_specs = (
        P("lam", None, "atom"),
        P("lam", None, "atom"),
        P("lam", None, "atom"),
        P(),
        P(),
        P(),
        P(),
        P("atom", None),
        P(),
    )
    out_specs = (
        P("lam", None),
        P("lam", None, "atom"),
        P("lam", None, "atom"),
        P("lam", None, "atom"),
    )
    return jax.shard_map(
        per_device, mesh=mesh, in_specs=in_specs, out_specs=out_specs, check_vma=False
    )
```

profile of v0, /device:TPU:8, one launch (start us, length us, event | category | flops | bytes accessed | tf_op | source)
XLA Modules:
  0.0 247.4 jit_solution(2960023894469162388)
XLA Ops:
  1.6 9.3 %collective-permute-start.1 = (f32[3,8192]{1,0:T(4,128)S(1)}, f32[3,8192]{1,0:T(4,128)S(1)}, u32[]{:S(2)}, u32[]{:S(2)}) collective-permute-start(f32[3,8192]{1,0:T(4,128)S(1)} %bitcast.218), channel_id=1, source_target_pairs={{0,254},{2,0},{4,2},{6,4},{8,6},{10,8},{12,10},{14,12},{16,14},{18... | collective-permute-start | bytes 294920 | tf_op jit(solution)/shard_map/ppermute | solution.py:26
  12.0 7.5 %collective-permute-start.4 = (f32[3,8192]{1,0:T(4,128)S(1)}, f32[3,8192]{1,0:T(4,128)}, u32[]{:S(2)}, u32[]{:S(2)}) collective-permute-start(f32[3,8192]{1,0:T(4,128)S(1)} %bitcast.226), channel_id=1, source_target_pairs={{0,254},{2,0},{4,2},{6,4},{8,6},{10,8},{12,10},{14,12},{16,14},{18... | collective-permute-start | bytes 294920 | tf_op jit(solution)/shard_map/ppermute | solution.py:26
  22.4 7.0 %all_gather.6 = f32[5,16384]{1,0:T(8,128)S(1)} all-gather(f32[5,8192]{1,0:T(8,128)S(1)} %pad_maximum_fusion), channel_id=1, replica_groups=mesh['lam'=128,'atom'=2] {'atom'}, dimensions={1}, use_global_device_ids=true | all-gather | bytes 491520 | tf_op jit(solution)/shard_map/all_gather | solution.py:21
  30.7 2.0 gather_fusion
  33.0 2.0 gather_fusion.1
  35.1 72.8 %while.32 = (s32[]{:T(128)}, f32[16]{0:T(128)S(1)}, f32[16,3,4,128]{3,2,1,0:T(4,128)S(1)}, s32[16,4,128]{2,1,0:T(4,128)S(1)}, s32[16,4,5,128]{3,2,1,0:T(8,128)S(...) while((s32[]{:T(128)}, f32[16]{0:T(128)S(1)}, ...), condition=%wide.region_4.5_spmd, body=%wide.region_0.4_spmd.sunk | while | flops 17365508 | bytes 5617881 | solution.py:108
  35.8 2.5 %compare_select_fusion.4 = (f32[4,5,128,128]{3,2,1,0:T(8,128)S(1)}, f32[]{:T(128)}) fusion(f32[4,5,128,128]{3,2,1,0:T(8,128)S(1)} %fusion.50, f32[4,5,128]{2,1,0:T(8,128)S(1)} %get-tuple-element.473, f32[4,128]{1,0:T(4,128)S(1)} %get-tuple-element.474, f32[4,5,128]{2,1,0:T(8,128)S(1)} %get-tuple-element.475, f32[4,128]{1,0:T(4,128)S(1)} %get-tuple-element.476, ...), kind=kLoop, calls=%fused_computation.17.clone.1 | loop fusion | flops 11796479 | bytes 2670596 | tf_op jit(solution)/shard_map/while/body/eval_jaxpr/mul | solution.py:80
  40.3 2.5 %compare_select_fusion.4 = (f32[4,5,128,128]{3,2,1,0:T(8,128)S(1)}, f32[]{:T(128)}) fusion(f32[4,5,128,128]{3,2,1,0:T(8,128)S(1)} %fusion.50, f32[4,5,128]{2,1,0:T(8,128)S(1)} %get-tuple-element.473, f32[4,128]{1,0:T(4,128)S(1)} %get-tuple-element.474, f32[4,5,128]{2,1,0:T(8,128)S(1)} %get-tuple-element.475, f32[4,128]{1,0:T(4,128)S(1)} %get-tuple-element.476, ...), kind=kLoop, calls=%fused_computation.17.clone.1 | loop fusion | flops 11796479 | bytes 2670596 | tf_op jit(solution)/shard_map/while/body/eval_jaxpr/mul | solution.py:80
  44.8 2.5 %compare_select_fusion.4 = (f32[4,5,128,128]{3,2,1,0:T(8,128)S(1)}, f32[]{:T(128)}) fusion(f32[4,5,128,128]{3,2,1,0:T(8,128)S(1)} %fusion.50, f32[4,5,128]{2,1,0:T(8,128)S(1)} %get-tuple-element.473, f32[4,128]{1,0:T(4,128)S(1)} %get-tuple-element.474, f32[4,5,128]{2,1,0:T(8,128)S(1)} %get-tuple-element.475, f32[4,128]{1,0:T(4,128)S(1)} %get-tuple-element.476, ...), kind=kLoop, calls=%fused_computation.17.clone.1 | loop fusion | flops 11796479 | bytes 2670596 | tf_op jit(solution)/shard_map/while/body/eval_jaxpr/mul | solution.py:80
  49.4 2.5 %compare_select_fusion.4 = (f32[4,5,128,128]{3,2,1,0:T(8,128)S(1)}, f32[]{:T(128)}) fusion(f32[4,5,128,128]{3,2,1,0:T(8,128)S(1)} %fusion.50, f32[4,5,128]{2,1,0:T(8,128)S(1)} %get-tuple-element.473, f32[4,128]{1,0:T(4,128)S(1)} %get-tuple-element.474, f32[4,5,128]{2,1,0:T(8,128)S(1)} %get-tuple-element.475, f32[4,128]{1,0:T(4,128)S(1)} %get-tuple-element.476, ...), kind=kLoop, calls=%fused_computation.17.clone.1 | loop fusion | flops 11796479 | bytes 2670596 | tf_op jit(solution)/shard_map/while/body/eval_jaxpr/mul | solution.py:80
  53.9 2.5 %compare_select_fusion.4 = (f32[4,5,128,128]{3,2,1,0:T(8,128)S(1)}, f32[]{:T(128)}) fusion(f32[4,5,128,128]{3,2,1,0:T(8,128)S(1)} %fusion.50, f32[4,5,128]{2,1,0:T(8,128)S(1)} %get-tuple-element.473, f32[4,128]{1,0:T(4,128)S(1)} %get-tuple-element.474, f32[4,5,128]{2,1,0:T(8,128)S(1)} %get-tuple-element.475, f32[4,128]{1,0:T(4,128)S(1)} %get-tuple-element.476, ...), kind=kLoop, calls=%fused_computation.17.clone.1 | loop fusion | flops 11796479 | bytes 2670596 | tf_op jit(solution)/shard_map/while/body/eval_jaxpr/mul | solution.py:80
  58.5 2.5 %compare_select_fusion.4 = (f32[4,5,128,128]{3,2,1,0:T(8,128)S(1)}, f32[]{:T(128)}) fusion(f32[4,5,128,128]{3,2,1,0:T(8,128)S(1)} %fusion.50, f32[4,5,128]{2,1,0:T(8,128)S(1)} %get-tuple-element.473, f32[4,128]{1,0:T(4,128)S(1)} %get-tuple-element.474, f32[4,5,128]{2,1,0:T(8,128)S(1)} %get-tuple-element.475, f32[4,128]{1,0:T(4,128)S(1)} %get-tuple-element.476, ...), kind=kLoop, calls=%fused_computation.17.clone.1 | loop fusion | flops 11796479 | bytes 2670596 | tf_op jit(solution)/shard_map/while/body/eval_jaxpr/mul | solution.py:80
  63.0 2.5 %compare_select_fusion.4 = (f32[4,5,128,128]{3,2,1,0:T(8,128)S(1)}, f32[]{:T(128)}) fusion(f32[4,5,128,128]{3,2,1,0:T(8,128)S(1)} %fusion.50, f32[4,5,128]{2,1,0:T(8,128)S(1)} %get-tuple-element.473, f32[4,128]{1,0:T(4,128)S(1)} %get-tuple-element.474, f32[4,5,128]{2,1,0:T(8,128)S(1)} %get-tuple-element.475, f32[4,128]{1,0:T(4,128)S(1)} %get-tuple-element.476, ...), kind=kLoop, calls=%fused_computation.17.clone.1 | loop fusion | flops 11796479 | bytes 2670596 | tf_op jit(solution)/shard_map/while/body/eval_jaxpr/mul | solution.py:80
  67.6 2.5 %compare_select_fusion.4 = (f32[4,5,128,128]{3,2,1,0:T(8,128)S(1)}, f32[]{:T(128)}) fusion(f32[4,5,128,128]{3,2,1,0:T(8,128)S(1)} %fusion.50, f32[4,5,128]{2,1,0:T(8,128)S(1)} %get-tuple-element.473, f32[4,128]{1,0:T(4,128)S(1)} %get-tuple-element.474, f32[4,5,128]{2,1,0:T(8,128)S(1)} %get-tuple-element.475, f32[4,128]{1,0:T(4,128)S(1)} %get-tuple-element.476, ...), kind=kLoop, calls=%fused_computation.17.clone.1 | loop fusion | flops 11796479 | bytes 2670596 | tf_op jit(solution)/shard_map/while/body/eval_jaxpr/mul | solution.py:80
  72.1 2.5 %compare_select_fusion.4 = (f32[4,5,128,128]{3,2,1,0:T(8,128)S(1)}, f32[]{:T(128)}) fusion(f32[4,5,128,128]{3,2,1,0:T(8,128)S(1)} %fusion.50, f32[4,5,128]{2,1,0:T(8,128)S(1)} %get-tuple-element.473, f32[4,128]{1,0:T(4,128)S(1)} %get-tuple-element.474, f32[4,5,128]{2,1,0:T(8,128)S(1)} %get-tuple-element.475, f32[4,128]{1,0:T(4,128)S(1)} %get-tuple-element.476, ...), kind=kLoop, calls=%fused_computation.17.clone.1 | loop fusion | flops 11796479 | bytes 2670596 | tf_op jit(solution)/shard_map/while/body/eval_jaxpr/mul | solution.py:80
  76.7 2.5 %compare_select_fusion.4 = (f32[4,5,128,128]{3,2,1,0:T(8,128)S(1)}, f32[]{:T(128)}) fusion(f32[4,5,128,128]{3,2,1,0:T(8,128)S(1)} %fusion.50, f32[4,5,128]{2,1,0:T(8,128)S(1)} %get-tuple-element.473, f32[4,128]{1,0:T(4,128)S(1)} %get-tuple-element.474, f32[4,5,128]{2,1,0:T(8,128)S(1)} %get-tuple-element.475, f32[4,128]{1,0:T(4,128)S(1)} %get-tuple-element.476, ...), kind=kLoop, calls=%fused_computation.17.clone.1 | loop fusion | flops 11796479 | bytes 2670596 | tf_op jit(solution)/shard_map/while/body/eval_jaxpr/mul | solution.py:80
  81.2 2.5 %compare_select_fusion.4 = (f32[4,5,128,128]{3,2,1,0:T(8,128)S(1)}, f32[]{:T(128)}) fusion(f32[4,5,128,128]{3,2,1,0:T(8,128)S(1)} %fusion.50, f32[4,5,128]{2,1,0:T(8,128)S(1)} %get-tuple-element.473, f32[4,128]{1,0:T(4,128)S(1)} %get-tuple-element.474, f32[4,5,128]{2,1,0:T(8,128)S(1)} %get-tuple-element.475, f32[4,128]{1,0:T(4,128)S(1)} %get-tuple-element.476, ...), kind=kLoop, calls=%fused_computation.17.clone.1 | loop fusion | flops 11796479 | bytes 2670596 | tf_op jit(solution)/shard_map/while/body/eval_jaxpr/mul | solution.py:80
  85.8 2.5 %compare_select_fusion.4 = (f32[4,5,128,128]{3,2,1,0:T(8,128)S(1)}, f32[]{:T(128)}) fusion(f32[4,5,128,128]{3,2,1,0:T(8,128)S(1)} %fusion.50, f32[4,5,128]{2,1,0:T(8,128)S(1)} %get-tuple-element.473, f32[4,128]{1,0:T(4,128)S(1)} %get-tuple-element.474, f32[4,5,128]{2,1,0:T(8,128)S(1)} %get-tuple-element.475, f32[4,128]{1,0:T(4,128)S(1)} %get-tuple-element.476, ...), kind=kLoop, calls=%fused_computation.17.clone.1 | loop fusion | flops 11796479 | bytes 2670596 | tf_op jit(solution)/shard_map/while/body/eval_jaxpr/mul | solution.py:80
  90.3 2.5 %compare_select_fusion.4 = (f32[4,5,128,128]{3,2,1,0:T(8,128)S(1)}, f32[]{:T(128)}) fusion(f32[4,5,128,128]{3,2,1,0:T(8,128)S(1)} %fusion.50, f32[4,5,128]{2,1,0:T(8,128)S(1)} %get-tuple-element.473, f32[4,128]{1,0:T(4,128)S(1)} %get-tuple-element.474, f32[4,5,128]{2,1,0:T(8,128)S(1)} %get-tuple-element.475, f32[4,128]{1,0:T(4,128)S(1)} %get-tuple-element.476, ...), kind=kLoop, calls=%fused_computation.17.clone.1 | loop fusion | flops 11796479 | bytes 2670596 | tf_op jit(solution)/shard_map/while/body/eval_jaxpr/mul | solution.py:80
  94.9 2.5 %compare_select_fusion.4 = (f32[4,5,128,128]{3,2,1,0:T(8,128)S(1)}, f32[]{:T(128)}) fusion(f32[4,5,128,128]{3,2,1,0:T(8,128)S(1)} %fusion.50, f32[4,5,128]{2,1,0:T(8,128)S(1)} %get-tuple-element.473, f32[4,128]{1,0:T(4,128)S(1)} %get-tuple-element.474, f32[4,5,128]{2,1,0:T(8,128)S(1)} %get-tuple-element.475, f32[4,128]{1,0:T(4,128)S(1)} %get-tuple-element.476, ...), kind=kLoop, calls=%fused_computation.17.clone.1 | loop fusion | flops 11796479 | bytes 2670596 | tf_op jit(solution)/shard_map/while/body/eval_jaxpr/mul | solution.py:80
  99.4 2.5 %compare_select_fusion.4 = (f32[4,5,128,128]{3,2,1,0:T(8,128)S(1)}, f32[]{:T(128)}) fusion(f32[4,5,128,128]{3,2,1,0:T(8,128)S(1)} %fusion.50, f32[4,5,128]{2,1,0:T(8,128)S(1)} %get-tuple-element.473, f32[4,128]{1,0:T(4,128)S(1)} %get-tuple-element.474, f32[4,5,128]{2,1,0:T(8,128)S(1)} %get-tuple-element.475, f32[4,128]{1,0:T(4,128)S(1)} %get-tuple-element.476, ...), kind=kLoop, calls=%fused_computation.17.clone.1 | loop fusion | flops 11796479 | bytes 2670596 | tf_op jit(solution)/shard_map/while/body/eval_jaxpr/mul | solution.py:80
  104.0 2.5 %compare_select_fusion.4 = (f32[4,5,128,128]{3,2,1,0:T(8,128)S(1)}, f32[]{:T(128)}) fusion(f32[4,5,128,128]{3,2,1,0:T(8,128)S(1)} %fusion.50, f32[4,5,128]{2,1,0:T(8,128)S(1)} %get-tuple-element.473, f32[4,128]{1,0:T(4,128)S(1)} %get-tuple-element.474, f32[4,5,128]{2,1,0:T(8,128)S(1)} %get-tuple-element.475, f32[4,128]{1,0:T(4,128)S(1)} %get-tuple-element.476, ...), kind=kLoop, calls=%fused_computation.17.clone.1 | loop fusion | flops 11796479 | bytes 2670596 | tf_op jit(solution)/shard_map/while/body/eval_jaxpr/mul | solution.py:80
  113.8 7.2 %all_gather.7 = f32[6,16384]{1,0:T(8,128)S(1)} all-gather(f32[6,8192]{1,0:T(8,128)S(1)} %pad_maximum_fusion.2), channel_id=1, replica_groups=mesh['lam'=128,'atom'=2] {'atom'}, dimensions={1}, use_global_device_ids=true | all-gather | bytes 589824 | tf_op jit(solution)/shard_map/all_gather | solution.py:21
  121.1 2.0 gather_fusion.2
  123.2 50.6 %while.33 = (s32[]{:T(128)}, f32[16]{0:T(128)S(1)}, s32[16,4,128]{2,1,0:T(4,128)S(1)}, s32[16,4,5,128]{3,2,1,0:T(8,128)S(1)}, f32[16,3,4,128]{3,2,1,0:T(4,128)S(...) while((s32[]{:T(128)}, f32[16]{0:T(128)S(1)}, ...), condition=%wide.region_9.10_spmd, body=%wide.region_6.9_spmd.sunk | while | flops 8847363 | bytes 2941133 | solution.py:108
  123.8 1.8 fusion.56
  127.0 1.8 fusion.56
  130.2 1.8 fusion.56
  133.3 1.8 fusion.56
  136.5 1.8 fusion.56
  139.6 1.8 fusion.56
  142.8 1.8 fusion.56
  146.0 1.8 fusion.56
  149.1 1.8 fusion.56
  152.3 1.8 fusion.56
  155.5 1.8 fusion.56
  158.6 1.8 fusion.56
  161.8 1.8 fusion.56
  164.9 1.8 fusion.56
  168.1 1.8 fusion.56
  171.3 1.8 fusion.56
  175.0 2.0 gather_fusion.3
  177.1 50.6 %while.34 = (s32[]{:T(128)}, f32[16]{0:T(128)S(1)}, s32[16,4,128]{2,1,0:T(4,128)S(1)}, s32[16,4,5,128]{3,2,1,0:T(8,128)S(1)}, f32[16,3,4,128]{3,2,1,0:T(4,128)S(...) while((s32[]{:T(128)}, f32[16]{0:T(128)S(1)}, ...), condition=%wide.region_14.15_spmd, body=%wide.region_11.14_spmd.sunk | while | flops 8847363 | bytes 2941133 | solution.py:108
  177.7 1.8 fusion.59
  180.9 1.8 fusion.59
  184.0 1.8 fusion.59
  187.2 1.8 fusion.59
  190.3 1.8 fusion.59
  193.5 1.8 fusion.59
  196.7 1.8 fusion.59
  199.8 1.8 fusion.59
  203.0 1.8 fusion.59
  206.2 1.8 fusion.59
  209.3 1.8 fusion.59
  212.5 1.8 fusion.59
  215.6 1.8 fusion.59
  218.8 1.8 fusion.59
  222.0 1.8 fusion.59
  225.1 1.8 fusion.59
  229.0 5.4 %all_to_all.6 = f32[2,1,3]{2,1,0:T(1,128)S(1)} all-to-all(f32[2,1,3]{2,1,0:T(1,128)S(1)} %broadcast_in_dim.37), channel_id=1, replica_groups=mesh['lam'=128,'atom'=2] {'atom'}, dimensions={0} | all-to-all | bytes 48 | tf_op jit(solution)/shard_map/all_to_all | solution.py:31
  235.1 1.0 collective-permute-start.3
  236.1 1.4 collective-permute-done.3
  237.6 7.3 %collective-permute-done.2 = f32[]{:T(128)} collective-permute-done((f32[]{:T(128)}, f32[]{:T(128)}, u32[]{:S(2)}, u32[]{:S(2)}) %collective-permute-start.2) | collective-permute-done | bytes 36 | tf_op jit(solution)/shard_map/ppermute | solution.py:26
  244.9 2.5 %maximum_bitcast_fusion = f32[1,3]{1,0:T(1,128)} fusion(f32[1]{0:T(128)} %bitcast.82, f32[1]{0:T(128)} %bitcast.80, f32[1]{0:T(128)} %get-tuple-element.313), kind=kLoop, calls=%fused_computation.122 | loop fusion | flops 6 | bytes 24 | tf_op jit(solution)/shard_map/broadcast_in_dim | solution.py:136
  (530 shorter events, 87.0 us)
Async XLA Ops:
  0.6 28.8 %copy-start.5 = (f32[16]{0:T(128)S(1)}, f32[16]{0:T(128)}, u32[]{:S(2)}) copy-start(f32[16]{0:T(128)} %param.20) | copy-start | bytes 196
  0.6 28.8 %copy-start.4 = (s32[16384]{0:T(1024)S(1)}, s32[16384]{0:T(1024)}, u32[]{:S(2)}) copy-start(s32[16384]{0:T(1024)} %param.19) | copy-start | bytes 196612
  1.6 110.1 %collective-permute-start.1 = (f32[3,8192]{1,0:T(4,128)S(1)}, f32[3,8192]{1,0:T(4,128)S(1)}, u32[]{:S(2)}, u32[]{:S(2)}) collective-permute-start(f32[3,8192]{1,0:T(4,128)S(1)} %bitcast.218), channel_id=1, source_target_pairs={{0,254},{2,0},{4,2},{6,4},{8,6},{10,8},{12,10},{14,12},{16,14},{18... | collective-permute-start | bytes 294920 | tf_op jit(solution)/shard_map/ppermute | solution.py:26
  10.9 100.8 %collective-permute-start = (f32[3,8192]{1,0:T(4,128)S(1)}, f32[3,8192]{1,0:T(4,128)S(1)}, u32[]{:S(2)}, u32[]{:S(2)}) collective-permute-start(f32[3,8192]{1,0:T(4,128)S(1)} %bitcast.219), channel_id=1, source_target_pairs={{0,2},{2,4},{4,6},{6,8},{8,10},{10,12},{12,14},{14,16},{16,18},{18... | collective-permute-start | bytes 294920 | tf_op jit(solution)/shard_map/ppermute | solution.py:26
  11.9 101.0 %collective-permute-start.5 = (f32[3,8192]{1,0:T(4,128)S(1)}, f32[3,8192]{1,0:T(4,128)}, u32[]{:S(2)}, u32[]{:S(2)}) collective-permute-start(f32[3,8192]{1,0:T(4,128)S(1)} %bitcast.225), channel_id=1, source_target_pairs={{0,2},{2,4},{4,6},{6,8},{8,10},{10,12},{12,14},{14,16},{16,18},{18... | collective-permute-start | bytes 294920 | tf_op jit(solution)/shard_map/ppermute | solution.py:26
  12.0 100.9 %collective-permute-start.4 = (f32[3,8192]{1,0:T(4,128)S(1)}, f32[3,8192]{1,0:T(4,128)}, u32[]{:S(2)}, u32[]{:S(2)}) collective-permute-start(f32[3,8192]{1,0:T(4,128)S(1)} %bitcast.226), channel_id=1, source_target_pairs={{0,254},{2,0},{4,2},{6,4},{8,6},{10,8},{12,10},{14,12},{16,14},{18... | collective-permute-start | bytes 294920 | tf_op jit(solution)/shard_map/ppermute | solution.py:26
  21.4 8.7 %copy-start.2 = (f32[16384]{0:T(1024)S(1)}, f32[16384]{0:T(1024)}, u32[]{:S(2)}) copy-start(f32[16384]{0:T(1024)} %param.18) | copy-start | bytes 196612
  33.0 2.1 copy-start
  35.1 72.8 %copy-start.3 = (s32[128]{0:T(128)S(1)}, s32[128]{0:T(128)}, u32[]{:S(2)}) copy-start(s32[128]{0:T(128)} %param.23) | copy-start | bytes 1540
  107.9 5.0 %copy-start.1 = (f32[1,3,8192]{2,0,1:T(1,128)S(1)}, f32[1,3,8192]{2,0,1:T(1,128)}, u32[]{:S(2)}) copy-start(f32[1,3,8192]{2,0,1:T(1,128)} %param.16) | copy-start | bytes 294916
  235.1 2.5 collective-permute-start.3
  236.1 8.7 %collective-permute-start.2 = (f32[]{:T(128)}, f32[]{:T(128)}, u32[]{:S(2)}, u32[]{:S(2)}) collective-permute-start(f32[]{:T(128)} %bitcast.79), channel_id=1, source_target_pairs={{0,2},{2,4},{4,6},{6,8},{8,10},{10,12},{12,14},{14,16},{16,18},{18... | collective-permute-start | bytes 20 | tf_op jit(solution)/shard_map/ppermute | solution.py:26
where the time goes:
time: 248 us; the launch traced here: 247 us
  other arithmetic  138 us (56%)
  local copies, waits for them, and re-layouts  56.2 us (23%)
  blocking collectives  19.7 us (8%)
  starting transfers between devices  18 us (7%)
  waiting for transfers between devices  8.73 us (4%)
  between operations  4.15 us (2%)
  loops' own time  2.52 us (1%)
    reduce_sum x32, other arithmetic, pair_block(): total = jnp.sum(energy_pair * pair_keep)  57.1 us
    mul x16, other arithmetic, pair_block(): weight = -2.0 * slope * pair_keep  39.9 us
    dynamic_update_slice x64, local copies, waits for them, and re-layouts, evaluate(): lax.map(partial(pair_block, with_force=with_force), (rows_pos, cols_pos,...  37.8 us
    reduce_sum x48, other arithmetic, pair_block(): squared = jnp.sum(delta * delta, axis=0)  22.5 us
    ppermute x6, starting transfers between devices, passed_along(): return lax.ppermute(x, axis, [(i, (i + by) % peers) for i in range(peers)])  18 us
    all_gather x2, blocking collectives, sent_together(): lax.all_gather(both, axis, axis=dim, tiled=True)  14.3 us
    reduce_sum x16, other arithmetic, pair_block(): force = jnp.sum(weight[None] * delta, axis=(2, 4))  11.1 us
    ppermute x6, waiting for transfers between devices, passed_along(): return lax.ppermute(x, axis, [(i, (i + by) % peers) for i in range(peers)])  8.73 us
  transfers between devices with their start and end apart: 6, of which 2 were waited for; matrix products, arithmetic and copies ran while one was open for 34% of the time, Pallas kernels for 0%

commit v1 on v0

v1 whole, which is shorter than its diff:
```python
from functools import partial

import jax
import jax.numpy as jnp
from jax import lax
from jax.experimental import pallas as pl
from jax.experimental.pallas import tpu as pltpu
from jax.sharding import PartitionSpec as P

TILE = 128
DELTA_SOFT = 0.05


def passed_along(x, axis, by):
    peers = lax.axis_size(axis)
    return lax.ppermute(x, axis, [(i, (i + by) % peers) for i in range(peers)])


def passed_across(x, by):
    cycle = lax.axis_size("lam")
    halves = lax.axis_size("atom")
    pairs = [
        (r * halves + a, ((r + by) % cycle) * halves + (a + 1) % halves)
        for r in range(cycle)
        for a in range(halves)
    ]
    return lax.ppermute(x, ("lam", "atom"), pairs)


def split3(z):
    one = z.astype(jnp.bfloat16)
    rest = z - one.astype(jnp.float32)
    two = rest.astype(jnp.bfloat16)
    rest = rest - two.astype(jnp.float32)
    return one, two, rest.astype(jnp.bfloat16)


def split2(z):
    one = z.astype(jnp.bfloat16)
    two = (z - one.astype(jnp.float32)).astype(jnp.bfloat16)
    return one, two


def tile_kernel(
    near_ref,
    pos_ref, cpl_ref, low_ref, up_ref,
    pos2_ref, cpl2_ref, low2_ref, up2_ref,
    look_ref,
    energy_ref, force_ref,
    feat_ref, side_ref, vec_ref, zc_ref, ze_ref,
    *, half, listed,
):
    first = near_ref[half * listed]

    def prepare(t, pos_from, cpl_from, low_from, up_from, own):
        lanes = pl.ds(pl.multiple_of(t * TILE, TILE), TILE)
        there = t + (first if own else half - first)
        dest = t if own else t + half
        looked = look_ref[:, pl.ds(pl.multiple_of(there * TILE, TILE), TILE)]
        pos = pos_from[:, lanes]
        charge0, depth0, h = looked[0:1], looked[1:2], looked[2:3]
        cpl, low, up = cpl_from[:, lanes], low_from[:, lanes], up_from[:, lanes]
        sq = pos * pos
        n = sq[0:1] + sq[1:2] + sq[2:3]
        h2 = h * h
        one = jnp.ones_like(n)
        zero = jnp.zeros_like(n)
        feats = jnp.concatenate([pos, n, h, h2, one, zero], axis=0)
        p1, p2, p3 = split3(feats)
        feat_ref[dest] = jnp.concatenate([p1, p1, p2, p2, p1, p3], axis=0)
        c0 = charge0 * cpl[0:1]
        e0 = depth0 * cpl[1:2]
        zc = jnp.concatenate(
            [c0, charge0 * low[0:1], charge0 * up[0:1], c0 * pos, zero, zero], axis=0
        )
        ze = jnp.concatenate(
            [e0, depth0 * low[1:2], depth0 * up[1:2], e0 * pos, zero, zero], axis=0
        )
        c1, c2 = split2(zc)
        e1, e2 = split2(ze)
        vec_ref[dest] = jnp.concatenate([c1, c2, e1, e2], axis=0)
        if own:
            zc_ref[dest] = zc
            ze_ref[dest] = ze
            m = -2.0 * pos
            hh = 2.0 * h
            sides = jnp.concatenate(
                [
                    jnp.concatenate([m, one, zero, zero, n + DELTA_SOFT, zero], axis=0),
                    jnp.concatenate([m, one, hh, one, n + h2, zero], axis=0),
                    jnp.concatenate([zero, zero, zero, zero, hh, one, h2, zero], axis=0),
                ],
                axis=1,
            )
            q1, q2, q3 = split3(sides)
            side_ref[dest] = jnp.concatenate([q1, q2, q1, q2, q3, q1], axis=0)

    def prep_own(t, _):
        prepare(t, pos_ref, cpl_ref, low_ref, up_ref, True)
        return 0

    def prep_other(t, _):
        prepare(t, pos2_ref, cpl2_ref, low2_ref, up2_ref, False)
        return 0

    lax.fori_loop(0, half, prep_own, 0)
    lax.fori_loop(0, half, prep_other, 0)

    def pair_sums(i, total):
        side = side_ref[i]
        acc = [jnp.zeros((16, TILE), jnp.float32) for _ in range(4)]
        own_times = jnp.int32(0)
        for k in range(listed):
            c = near_ref[i * listed + k]
            own_times = own_times + jnp.where(c == i, 1, 0)
            feat = feat_ref[c]
            vec = vec_ref[c]
            stg = lax.dot_general(
                feat, side, (((0,), (0,)), ((), ())), preferred_element_type=jnp.float32
            )
            s, t, g = stg[:, :TILE], stg[:, TILE : 2 * TILE], stg[:, 2 * TILE :]
            inv = lax.rsqrt(s)
            rt = 1.0 / t
            x = g * rt
            x3 = x * x * x
            p = x3 * (x3 - 0.5)
            b = x3 * (x3 - 1.0)
            f = p * rt
            inv3 = inv * inv * inv
            cc = jnp.concatenate([vec[:16], vec[:16]], axis=1)
            ee = jnp.concatenate([vec[16:], vec[16:]], axis=1)
            for n, (lhs, mat) in enumerate(((cc, inv), (ee, b), (cc, inv3), (ee, f))):
                hi, lo = split2(mat)
                acc[n] = acc[n] + jnp.dot(
                    lhs, jnp.concatenate([hi, lo], axis=0), preferred_element_type=jnp.float32
                )
        sum_a, sum_b, sum_i, sum_f = [a[:8] + a[8:] for a in acc]
        zc = zc_ref[i]
        ze = ze_ref[i]
        own = own_times.astype(jnp.float32) * (DELTA_SOFT**-0.5)
        total = total + zc * (sum_a - own * zc) + 4.0 * (ze * sum_b)
        lanes = pl.ds(pl.multiple_of(i * TILE, TILE), TILE)
        pos = pos_ref[:, lanes]
        force = zc[0:1] * (pos * sum_i[0:1] - sum_i[3:6]) + 48.0 * ze[0:1] * (
            pos * sum_f[0:1] - sum_f[3:6]
        )
        force_ref[:, lanes] = force
        return total

    total = lax.fori_loop(0, half, pair_sums, jnp.zeros((8, TILE), jnp.float32))
    energy_ref[...] = jnp.broadcast_to(jnp.sum(total, axis=1, keepdims=True), (8, TILE))


def lookup(charges, types, type_sigma, type_eps):
    levels = lax.broadcasted_iota(jnp.int32, (type_sigma.shape[0], types.shape[0]), 0)
    onehot = (levels == types[None, :]).astype(jnp.float32)
    table = jnp.stack([jnp.sqrt(type_eps), 0.5 * type_sigma])
    looked = jnp.dot(table, onehot, precision=lax.Precision.HIGHEST)
    return jnp.concatenate([charges[None], looked])


def call_kernel(args, half, listed):
    width = half * TILE
    tiles = 2 * half
    vmem = pl.BlockSpec(memory_space=pltpu.VMEM)
    return pl.pallas_call(
        partial(tile_kernel, half=half, listed=listed),
        out_shape=(
            jax.ShapeDtypeStruct((8, TILE), jnp.float32),
            jax.ShapeDtypeStruct((3, width), jnp.float32),
        ),
        in_specs=[pl.BlockSpec(memory_space=pltpu.SMEM)] + [vmem] * 9,
        out_specs=(vmem, vmem),
        scratch_shapes=[
            pltpu.VMEM((tiles, 48, TILE), jnp.bfloat16),
            pltpu.VMEM((half, 48, 3 * TILE), jnp.bfloat16),
            pltpu.VMEM((tiles, 32, TILE), jnp.bfloat16),
            pltpu.VMEM((half, 8, TILE), jnp.float32),
            pltpu.VMEM((half, 8, TILE), jnp.float32),
        ],
        compiler_params=pltpu.CompilerParams(vmem_limit_bytes=40 * 2**20),
        name="tiles",
    )(*args)


def per_device(
    coords, velocities, coupling, charges, types, type_sigma, type_eps, near_tiles, accept
):
    pos = coords[0]
    moving = velocities[0]
    cpl = coupling[0]
    width = pos.shape[1]
    half = width // TILE
    atoms = charges.shape[0]
    listed = near_tiles.shape[1]
    pos2 = passed_along(pos, "atom", 1)
    cpl2 = passed_along(cpl, "atom", 1)
    low = passed_along(cpl, "lam", 1)
    up = passed_along(cpl, "lam", -1)
    low2 = passed_across(cpl, 1)
    up2 = passed_across(cpl, -1)
    lower_coords, lower_moving = passed_along((pos, moving), "lam", 1)
    upper_coords, upper_moving = passed_along((pos, moving), "lam", -1)

    look = lookup(charges, types, type_sigma, type_eps)
    first = lax.axis_index("atom") * half
    tiles = 2 * half
    local = jnp.mod(near_tiles.reshape(-1) - first + tiles, tiles)
    near = jnp.concatenate([local, first[None]]).astype(jnp.int32)

    energy, force = call_kernel(
        (near, pos, cpl, low, up, pos2, cpl2, low2, up2, look), half, listed
    )

    part = energy[:3, 0] * (0.5 / atoms)
    energies = (part + passed_along(part, "atom", 1))[None]
    replica = lax.axis_index("lam")
    cycle_size = lax.axis_size("lam")
    upper_flag = accept[replica] == 1
    lower_flag = accept[(replica + cycle_size - 1) % cycle_size] == 1
    new_coords = jnp.where(upper_flag, upper_coords, jnp.where(lower_flag, lower_coords, pos))
    new_velocities = jnp.where(
        upper_flag, upper_moving, jnp.where(lower_flag, lower_moving, moving)
    )
    return (energies, force[None], new_coords[None], new_velocities[None])


def solution(mesh):
    in_specs = (
        P("lam", None, "atom"),
        P("lam", None, "atom"),
        P("lam", None, "atom"),
        P(),
        P(),
        P(),
        P(),
        P("atom", None),
        P(),
    )
    out_specs = (
        P("lam", None),
        P("lam", None, "atom"),
        P("lam", None, "atom"),
        P("lam", None, "atom"),
    )
    return jax.shard_map(
        per_device, mesh=mesh, in_specs=in_specs, out_specs=out_specs, check_vma=False
    )
```

time: 248 us -> 106 us (0.43)
  the two profiles are of different devices: /device:TPU:8 before, /device:TPU:119 now
where the time goes in v1:
time: 106 us
  Pallas kernels  67.7 us (64%)
  starting transfers between devices  29.5 us (28%)
  local copies, waits for them, and re-layouts  5.45 us (5%)
  between operations  2.09 us (2%)
  other arithmetic  1.06 us (1%)
    pallas_call x1, Pallas kernels, call_kernel(): pl.pallas_call(partial(tile_kernel, half=half, listed=listed), out_shape=...  67.7 us
    ppermute x9, starting transfers between devices, passed_along(): return lax.ppermute(x, axis, [(i, (i + by) % peers) for i in range(peers)])  23.3 us
    ppermute x2, starting transfers between devices, passed_across(): return lax.ppermute(x, ('lam', 'atom'), pairs)  6.13 us
    unnamed x23, local copies, waits for them, and re-layouts  4.63 us
  transfers between devices with their start and end apart: 11, of which 0 were waited for; matrix products, arithmetic and copies ran while one was open for 4% of the time, Pallas kernels for 64%

profile of v1, /device:TPU:119, one launch (start us, length us, event | category | flops | bytes accessed | tf_op | source)
XLA Modules:
  0.0 106.2 jit_solution(13721664063876734706)
XLA Ops:
  0.6 0.0 copy-start.4
  0.6 0.0 copy-start.8
  0.7 3.2 %collective-permute-start = (f32[2,8192]{1,0:T(2,128)}, f32[2,8192]{1,0:T(2,128)S(1)}, u32[]{:S(2)}, u32[]{:S(2)}) collective-permute-start(f32[2,8192]{1,0:T(2,128)} %bitcast.31), channel_id=1, source_target_pairs={{0,2},{2,4},{4,6},{6,8},{8,10},{10,12},{12,14},{14,16},{16,18},{18... | collective-permute-start | bytes 196616 | tf_op jit(solution)/shard_map/ppermute | solution.py:16
  3.8 0.0 collective-permute-start.1
  3.8 1.9 %collective-permute-start.3 = (f32[2,8192]{1,0:T(2,128)}, f32[2,8192]{1,0:T(2,128)S(1)}, u32[]{:S(2)}, u32[]{:S(2)}) collective-permute-start(f32[2,8192]{1,0:T(2,128)} %bitcast.33), channel_id=1, source_target_pairs={{0,1},{1,0},{2,3},{3,2},{4,5},{5,4},{6,7},{7,6},{8,9},{9,8},{10,11... | collective-permute-start | bytes 196616 | tf_op jit(solution)/shard_map/ppermute | solution.py:16
  5.7 6.1 %collective-permute-start.4 = (f32[2,8192]{1,0:T(2,128)}, f32[2,8192]{1,0:T(2,128)S(1)}, u32[]{:S(2)}, u32[]{:S(2)}) collective-permute-start(f32[2,8192]{1,0:T(2,128)} %bitcast.34), channel_id=1, source_target_pairs={{0,3},{1,2},{2,5},{3,4},{4,7},{5,6},{6,9},{7,8},{8,11},{9,10},{10,... | collective-permute-start | bytes 196616 | tf_op jit(solution)/shard_map/ppermute | solution.py:27
  11.9 0.0 collective-permute-start.5
  11.9 0.0 copy-done.4
  11.9 0.1 copy.16
  12.0 0.0 copy-start.6
  12.0 0.0 copy-start.7
  12.0 0.1 add.36
  12.1 0.5 copy-done.6
  12.6 0.0 copy-done.7
  12.6 0.0 copy-done.8
  12.7 0.0 copy-start.3
  12.7 0.4 fusion
  13.1 0.4 copy-done.3
  13.5 0.0 copy-start.1
  13.5 0.1 pad_maximum_fusion.look_ref
  13.7 0.7 copy-done.1
  14.4 0.0 copy-start.5
  14.4 0.0 copy-start.2
  14.4 0.1 copy.29
  14.5 0.6 copy-done.5
  15.0 0.6 fusion.7
  16.9 0.0 copy-done.2
  16.9 0.0 copy-start
  17.0 0.1 copy.28
  17.0 0.0 collective-permute-done.low_ref
  17.0 2.0 %collective-permute-start.2 = (f32[3,8192]{1,0:T(4,128)S(1)}, f32[3,8192]{1,0:T(4,128)S(1)}, u32[]{:S(2)}, u32[]{:S(2)}) collective-permute-start(f32[3,8192]{1,0:T(4,128)S(1)} %bitcast.26), channel_id=1, source_target_pairs={{0,1},{1,0},{2,3},{3,2},{4,5},{5,4},{6,7},{7,6},{8,9},{9,8},{10,11... | collective-permute-start | bytes 294920 | tf_op jit(solution)/shard_map/ppermute | solution.py:16
  19.0 0.1 pad_add_fusion.near_ref
  19.1 0.0 collective-permute-done.1.up_ref
  19.1 0.0 collective-permute-start.7
  19.1 0.0 collective-permute-done.3.cpl2_ref
  19.1 7.4 %collective-permute-start.8 = (f32[3,8192]{1,0:T(4,128)S(1)}, f32[3,8192]{1,0:T(4,128)S(1)}, u32[]{:S(2)}, u32[]{:S(2)}) collective-permute-start(f32[3,8192]{1,0:T(4,128)S(1)} %bitcast.28), channel_id=1, source_target_pairs={{0,2},{2,4},{4,6},{6,8},{8,10},{10,12},{12,14},{14,16},{16,18},{18... | collective-permute-start | bytes 294920 | tf_op jit(solution)/shard_map/ppermute | solution.py:16
  26.6 0.0 collective-permute-done.4.low2_ref
  26.6 0.0 collective-permute-start.9
  26.6 0.0 collective-permute-done.5.up2_ref
  26.6 7.5 %collective-permute-start.10 = (f32[3,8192]{1,0:T(4,128)S(1)}, f32[3,8192]{1,0:T(4,128)S(1)}, u32[]{:S(2)}, u32[]{:S(2)}) collective-permute-start(f32[3,8192]{1,0:T(4,128)S(1)} %bitcast.38), channel_id=1, source_target_pairs={{0,2},{2,4},{4,6},{6,8},{8,10},{10,12},{12,14},{14,16},{16,18},{18... | collective-permute-start | bytes 294920 | tf_op jit(solution)/shard_map/ppermute | solution.py:16
  34.1 0.0 collective-permute-done.2.pos2_ref
  34.1 0.0 copy-done
  34.1 67.7 %tiles.1 = (f32[8,128]{1,0:T(8,128)S(1)}, f32[3,8192]{1,0:T(4,128)S(1)}) custom-call(s32[321]{0:T(512)S(1)} %pad_add_fusion.near_ref, f32[3,8192]{1,0:T(4,128)S(1)} %bitcast.29, f32[2,8192]{1,0:T(2,128)S(1)} %bitcast.36, f32[2,8192]{1,0:T(2,128)S(1)} %collective-permute-done.low_ref, f32[2,8192]{1,0:T(2,128)S(1)} %collective-permute-done.1.up_ref, ...), custom_call_target="tpu_custom_call" | custom-call | tf_op jit(solution)/shard_map/tiles/pallas_call | solution.py:166
  101.8 0.1 multiply_reduce_fusion
  101.9 1.3 %collective-permute-start.6 = (f32[3]{0:T(128)S(1)}, f32[3]{0:T(128)S(1)}, u32[]{:S(2)}, u32[]{:S(2)}) collective-permute-start(f32[3]{0:T(128)S(1)} %multiply_reduce_fusion), channel_id=1, source_target_pairs={{0,1},{1,0},{2,3},{3,2},{4,5},{5,4},{6,7},{7,6},{8,9},{9,8},{10,11... | collective-permute-start | bytes 44 | tf_op jit(solution)/shard_map/ppermute | solution.py:16
  103.3 0.0 collective-permute-done.7
  103.3 0.0 collective-permute-done.8
  103.3 0.1 select_bitcast_fusion.1
  103.4 0.7 copy.17
  104.1 0.7 copy.18
  104.9 0.0 collective-permute-done.9
  104.9 0.0 collective-permute-done.10
  104.9 0.1 select_bitcast_fusion
  105.0 0.7 copy.19
  105.7 0.0 collective-permute-done.6
  105.7 0.5 add_bitcast_fusion
  (3 shorter events, 0.0 us)
Async XLA Ops:
  0.6 11.2 %copy-start.4 = (s32[64,5]{0,1:T(8,128)S(1)}, s32[64,5]{0,1:T(8,128)}, u32[]{:S(2)}) copy-start(s32[64,5]{0,1:T(8,128)} %param.16) | copy-start | bytes 3844
  0.6 12.0 %copy-start.8 = (s32[16384]{0:T(1024)S(1)}, s32[16384]{0:T(1024)}, u32[]{:S(2)}) copy-start(s32[16384]{0:T(1024)} %param.13) | copy-start | bytes 196612
  0.7 16.4 %collective-permute-start = (f32[2,8192]{1,0:T(2,128)}, f32[2,8192]{1,0:T(2,128)S(1)}, u32[]{:S(2)}, u32[]{:S(2)}) collective-permute-start(f32[2,8192]{1,0:T(2,128)} %bitcast.31), channel_id=1, source_target_pairs={{0,2},{2,4},{4,6},{6,8},{8,10},{10,12},{12,14},{14,16},{16,18},{18... | collective-permute-start | bytes 196616 | tf_op jit(solution)/shard_map/ppermute | solution.py:16
  3.8 15.3 %collective-permute-start.1 = (f32[2,8192]{1,0:T(2,128)}, f32[2,8192]{1,0:T(2,128)S(1)}, u32[]{:S(2)}, u32[]{:S(2)}) collective-permute-start(f32[2,8192]{1,0:T(2,128)} %bitcast.32), channel_id=1, source_target_pairs={{0,254},{2,0},{4,2},{6,4},{8,6},{10,8},{12,10},{14,12},{16,14},{18... | collective-permute-start | bytes 196616 | tf_op jit(solution)/shard_map/ppermute | solution.py:16
  3.8 15.3 %collective-permute-start.3 = (f32[2,8192]{1,0:T(2,128)}, f32[2,8192]{1,0:T(2,128)S(1)}, u32[]{:S(2)}, u32[]{:S(2)}) collective-permute-start(f32[2,8192]{1,0:T(2,128)} %bitcast.33), channel_id=1, source_target_pairs={{0,1},{1,0},{2,3},{3,2},{4,5},{5,4},{6,7},{7,6},{8,9},{9,8},{10,11... | collective-permute-start | bytes 196616 | tf_op jit(solution)/shard_map/ppermute | solution.py:16
  5.7 20.9 %collective-permute-start.4 = (f32[2,8192]{1,0:T(2,128)}, f32[2,8192]{1,0:T(2,128)S(1)}, u32[]{:S(2)}, u32[]{:S(2)}) collective-permute-start(f32[2,8192]{1,0:T(2,128)} %bitcast.34), channel_id=1, source_target_pairs={{0,3},{1,2},{2,5},{3,4},{4,7},{5,6},{6,9},{7,8},{8,11},{9,10},{10,... | collective-permute-start | bytes 196616 | tf_op jit(solution)/shard_map/ppermute | solution.py:27
  11.9 14.7 %collective-permute-start.5 = (f32[2,8192]{1,0:T(2,128)}, f32[2,8192]{1,0:T(2,128)S(1)}, u32[]{:S(2)}, u32[]{:S(2)}) collective-permute-start(f32[2,8192]{1,0:T(2,128)} %bitcast.35), channel_id=1, source_target_pairs={{0,255},{1,254},{2,1},{3,0},{4,3},{5,2},{6,5},{7,4},{8,7},{9,6},{1... | collective-permute-start | bytes 196616 | tf_op jit(solution)/shard_map/ppermute | solution.py:27
  12.0 0.7 copy-start.6
  12.0 0.7 copy-start.7
  12.7 0.8 copy-start.3
  13.5 0.9 copy-start.1
  14.4 0.7 copy-start.5
  14.4 2.5 %copy-start.2 = (f32[1,3,8192]{2,0,1:T(1,128)S(1)}, f32[1,3,8192]{2,0,1:T(1,128)}, u32[]{:S(2)}) copy-start(f32[1,3,8192]{2,0,1:T(1,128)} %param.10) | copy-start | bytes 294916
  16.9 17.1 %copy-start = (f32[1,2,8192]{2,1,0:T(2,128)S(1)}, f32[1,2,8192]{2,1,0:T(2,128)}, u32[]{:S(2)}) copy-start(f32[1,2,8192]{2,1,0:T(2,128)} %param.11) | copy-start | bytes 196612
  17.0 17.0 %collective-permute-start.2 = (f32[3,8192]{1,0:T(4,128)S(1)}, f32[3,8192]{1,0:T(4,128)S(1)}, u32[]{:S(2)}, u32[]{:S(2)}) collective-permute-start(f32[3,8192]{1,0:T(4,128)S(1)} %bitcast.26), channel_id=1, source_target_pairs={{0,1},{1,0},{2,3},{3,2},{4,5},{5,4},{6,7},{7,6},{8,9},{9,8},{10,11... | collective-permute-start | bytes 294920 | tf_op jit(solution)/shard_map/ppermute | solution.py:16
  19.1 84.2 %collective-permute-start.7 = (f32[3,8192]{1,0:T(4,128)S(1)}, f32[3,8192]{1,0:T(4,128)S(1)}, u32[]{:S(2)}, u32[]{:S(2)}) collective-permute-start(f32[3,8192]{1,0:T(4,128)S(1)} %bitcast.27), channel_id=1, source_target_pairs={{0,254},{2,0},{4,2},{6,4},{8,6},{10,8},{12,10},{14,12},{16,14},{18... | collective-permute-start | bytes 294920 | tf_op jit(solution)/shard_map/ppermute | solution.py:16
  19.1 84.1 %collective-permute-start.8 = (f32[3,8192]{1,0:T(4,128)S(1)}, f32[3,8192]{1,0:T(4,128)S(1)}, u32[]{:S(2)}, u32[]{:S(2)}) collective-permute-start(f32[3,8192]{1,0:T(4,128)S(1)} %bitcast.28), channel_id=1, source_target_pairs={{0,2},{2,4},{4,6},{6,8},{8,10},{10,12},{12,14},{14,16},{16,18},{18... | collective-permute-start | bytes 294920 | tf_op jit(solution)/shard_map/ppermute | solution.py:16
  26.6 78.3 %collective-permute-start.9 = (f32[3,8192]{1,0:T(4,128)S(1)}, f32[3,8192]{1,0:T(4,128)S(1)}, u32[]{:S(2)}, u32[]{:S(2)}) collective-permute-start(f32[3,8192]{1,0:T(4,128)S(1)} %bitcast.37), channel_id=1, source_target_pairs={{0,254},{2,0},{4,2},{6,4},{8,6},{10,8},{12,10},{14,12},{16,14},{18... | collective-permute-start | bytes 294920 | tf_op jit(solution)/shard_map/ppermute | solution.py:16
  26.6 78.3 %collective-permute-start.10 = (f32[3,8192]{1,0:T(4,128)S(1)}, f32[3,8192]{1,0:T(4,128)S(1)}, u32[]{:S(2)}, u32[]{:S(2)}) collective-permute-start(f32[3,8192]{1,0:T(4,128)S(1)} %bitcast.38), channel_id=1, source_target_pairs={{0,2},{2,4},{4,6},{6,8},{8,10},{10,12},{12,14},{14,16},{16,18},{18... | collective-permute-start | bytes 294920 | tf_op jit(solution)/shard_map/ppermute | solution.py:16
  101.9 3.8 %collective-permute-start.6 = (f32[3]{0:T(128)S(1)}, f32[3]{0:T(128)S(1)}, u32[]{:S(2)}, u32[]{:S(2)}) collective-permute-start(f32[3]{0:T(128)S(1)} %multiply_reduce_fusion), channel_id=1, source_target_pairs={{0,1},{1,0},{2,3},{3,2},{4,5},{5,4},{6,7},{7,6},{8,9},{9,8},{10,11... | collective-permute-start | bytes 44 | tf_op jit(solution)/shard_map/ppermute | solution.py:16

commit v2 on v1

v2 whole, which is shorter than its diff:
```python
from functools import partial

import jax
import jax.numpy as jnp
from jax import lax
from jax.experimental import pallas as pl
from jax.experimental.pallas import tpu as pltpu
from jax.sharding import PartitionSpec as P

TILE = 128
DELTA_SOFT = 0.05
CHUNK = 32
RING = 5
AHEAD = 3
LATE = 2
ROWS = 4


def swapped(x, axis, first):
    peers = lax.axis_size(axis)
    pairs = []
    for i in range(first, peers + first, 2):
        low, high = i % peers, (i + 1) % peers
        pairs += [(low, high), (high, low)]
    return lax.ppermute(x, axis, pairs)


def split3(z):
    one = z.astype(jnp.bfloat16)
    rest = z - one.astype(jnp.float32)
    two = rest.astype(jnp.bfloat16)
    rest = rest - two.astype(jnp.float32)
    return one, two, rest.astype(jnp.bfloat16)


def split2(z):
    one = z.astype(jnp.bfloat16)
    two = (z - one.astype(jnp.float32)).astype(jnp.bfloat16)
    return one, two


def tile_kernel(
    near_ref,
    five_ref, moving_ref, other_ref, pair1_ref, pair2_ref, look_ref,
    energy_ref, force_ref, coords_out, moving_out,
    feat_ref, side_ref, vec_ref, zc_ref, ze_ref, pos_ref, new_ref, sem, *work_refs,
    half, listed,
):
    first = near_ref[half * listed]
    take1 = near_ref[half * listed + 1] == 1
    take2 = near_ref[half * listed + 2] == 1
    dist_refs, mat_refs = work_refs[:RING], work_refs[RING:]

    def prepare(t, from_ref, at, own):
        def rows(ref, *js):
            return [ref[j, pl.ds(t, 1), :] for j in js]

        there = t + (first if own else half - first)
        dest = t if own else t + half
        charge0, depth0, h = [look_ref[j, pl.ds(there, 1), :] for j in range(3)]
        x, y, z, cpl0, cpl1 = rows(from_ref, *range(5))
        low0, low1 = rows(pair1_ref, at, at + 1)
        up0, up1 = rows(pair2_ref, at, at + 1)
        n = x * x + y * y + z * z
        h2 = h * h
        one = jnp.ones_like(n)
        zero = jnp.zeros_like(n)
        feats = jnp.concatenate([x, y, z, n, h, h2, one, zero], axis=0)
        p1, p2, p3 = split3(feats)
        feat_ref[dest] = jnp.concatenate([p1, p1, p2, p2, p1, p3], axis=0)
        c0 = charge0 * cpl0
        e0 = depth0 * cpl1
        pos = feats[0:3]
        zc = jnp.concatenate([c0, charge0 * low0, charge0 * up0, c0 * pos, zero, zero], axis=0)
        ze = jnp.concatenate([e0, depth0 * low1, depth0 * up1, e0 * pos, zero, zero], axis=0)
        c1, c2 = split2(zc)
        e1, e2 = split2(ze)
        vec_ref[dest] = jnp.concatenate([c1, c2, e1, e2], axis=0)
        if own:
            zc_ref[dest] = zc
            ze_ref[dest] = ze
            pos_ref[dest] = feats
            m = -2.0 * pos
            hh = 2.0 * h
            sides = jnp.concatenate(
                [
                    jnp.concatenate([m, one, zero, zero, n + DELTA_SOFT, zero], axis=0),
                    jnp.concatenate([m, one, hh, one, n + h2, zero], axis=0),
                    jnp.concatenate([zero, zero, zero, zero, hh, one, h2, zero], axis=0),
                ],
                axis=1,
            )
            q1, q2, q3 = split3(sides)
            side_ref[dest] = jnp.concatenate([q1, q2, q1, q2, q3, q1], axis=0)
            lanes = pl.ds(pl.multiple_of(t * TILE, TILE), TILE)
            own_rows = [x, y, z] + rows(moving_ref, *range(3))
            for n, (mine, one_row, two_row) in enumerate(
                zip(own_rows, rows(pair1_ref, *range(4, 10)), rows(pair2_ref, *range(4, 10)))
            ):
                new_ref[n // 3, pl.ds(n % 3, 1), lanes] = jnp.where(
                    take1, one_row, jnp.where(take2, two_row, mine)
                )

    def prep_own(t, _):
        prepare(t, five_ref, 0, True)
        return 0

    def prep_other(t, _):
        prepare(t, other_ref, 2, False)
        return 0

    lax.fori_loop(0, half, prep_own, 0)
    copies = [
        pltpu.make_async_copy(new_ref.at[n], out, sem.at[n])
        for n, out in enumerate((coords_out, moving_out))
    ]
    for copy in copies:
        copy.start()
    lax.fori_loop(0, half, prep_other, 0)

    def distances(i, k):
        c = near_ref[i * listed + k]
        dist_refs[k % RING][...] = lax.dot_general(
            feat_ref[c], side_ref[i], (((0,), (0,)), ((), ())),
            preferred_element_type=jnp.float32,
        )

    def functions(k):
        dist_ref, mat_ref = dist_refs[k % RING], mat_refs[k % RING]
        for r in range(0, TILE, CHUNK):
            rows = slice(r, r + CHUNK)
            low_rows = slice(TILE + r, TILE + r + CHUNK)
            s = dist_ref[rows, :TILE]
            t = dist_ref[rows, TILE : 2 * TILE]
            g = dist_ref[rows, 2 * TILE :]
            inv = lax.rsqrt(s)
            rt = 1.0 / t
            x = g * rt
            x3 = x * x * x
            f = x3 * (x3 - 0.5) * rt
            b = x3 * (x3 - 1.0)
            for n, mat in enumerate((inv, b, inv * inv * inv, f)):
                hi, lo = split2(mat)
                mat_ref[n, rows] = hi
                mat_ref[n, low_rows] = lo

    def gather(i, k, acc):
        vec = vec_ref[near_ref[i * listed + k]]
        cc = jnp.concatenate([vec[:16], vec[:16]], axis=1)
        ee = jnp.concatenate([vec[16:], vec[16:]], axis=1)
        mat_ref = mat_refs[k % RING]
        return [
            a + jnp.dot(lhs, mat_ref[n], preferred_element_type=jnp.float32)
            for n, (a, lhs) in enumerate(zip(acc, (cc, ee, cc, ee)))
        ]

    def finish(i, acc, total):
        sum_a, sum_b, sum_i, sum_f = [a[:8] + a[8:] for a in acc]
        own_times = jnp.int32(0)
        for k in range(listed):
            own_times = own_times + jnp.where(near_ref[i * listed + k] == i, 1, 0)
        zc = zc_ref[i]
        ze = ze_ref[i]
        own = own_times.astype(jnp.float32) * (DELTA_SOFT**-0.5)
        lanes = pl.ds(pl.multiple_of(i * TILE, TILE), TILE)
        pos = pos_ref[i, 0:3]
        force_ref[:, lanes] = zc[0:1] * (pos * sum_i[0:1] - sum_i[3:6]) + 48.0 * ze[0:1] * (
            pos * sum_f[0:1] - sum_f[3:6]
        )
        return total + zc * (sum_a - own * zc) + 4.0 * (ze * sum_b)

    def nothing():
        return [jnp.zeros((16, TILE), jnp.float32) for _ in range(4)]

    def row(i, acc, total):
        behind = jnp.maximum(i - 1, 0)
        following = jnp.minimum(i + 1, half - 1)
        for k in range(listed - LATE, listed):
            acc = gather(behind, k, acc)
        done = finish(behind, acc, total)
        total = jnp.where(i > 0, done, total)
        acc = nothing()
        for k in range(listed):
            if k + AHEAD < listed:
                distances(i, k + AHEAD)
            functions(k)
            if k + AHEAD >= listed:
                distances(following, k + AHEAD - listed)
            if k < listed - LATE:
                acc = gather(i, k, acc)
        return acc, total

    def next_rows(step, carry):
        for j in range(ROWS):
            carry = row(step * ROWS + j, *carry)
        return carry

    for k in range(AHEAD):
        distances(0, k)
    for k in range(listed - LATE, listed):
        mat_refs[k][...] = jnp.zeros_like(mat_refs[k])
    acc, total = lax.fori_loop(
        0, half // ROWS, next_rows, (nothing(), jnp.zeros((8, TILE), jnp.float32))
    )
    for k in range(listed - LATE, listed):
        acc = gather(half - 1, k, acc)
    total = finish(half - 1, acc, total)
    energy_ref[...] = jnp.broadcast_to(jnp.sum(total, axis=1, keepdims=True), (8, TILE))
    for copy in copies:
        copy.wait()


def lookup(charges, types, type_sigma, type_eps):
    levels = lax.broadcasted_iota(jnp.int32, (type_sigma.shape[0], types.shape[0]), 0)
    onehot = (levels == types[None, :]).astype(jnp.float32)
    table = jnp.stack([jnp.sqrt(type_eps), 0.5 * type_sigma])
    looked = jnp.dot(table, onehot, precision=lax.Precision.HIGHEST)
    return jnp.concatenate([charges[None], looked])


def call_kernel(args, half, listed):
    width = half * TILE
    tiles = 2 * half
    vmem = pl.BlockSpec(memory_space=pltpu.VMEM)
    hbm = pl.BlockSpec(memory_space=pltpu.HBM)
    return pl.pallas_call(
        partial(tile_kernel, half=half, listed=listed),
        out_shape=(
            jax.ShapeDtypeStruct((8, TILE), jnp.float32),
            jax.ShapeDtypeStruct((3, width), jnp.float32),
            jax.ShapeDtypeStruct((3, width), jnp.float32),
            jax.ShapeDtypeStruct((3, width), jnp.float32),
        ),
        in_specs=[pl.BlockSpec(memory_space=pltpu.SMEM)] + [vmem] * 6,
        out_specs=(vmem, vmem, hbm, hbm),
        scratch_shapes=[
            pltpu.VMEM((tiles, 48, TILE), jnp.bfloat16),
            pltpu.VMEM((half, 48, 3 * TILE), jnp.bfloat16),
            pltpu.VMEM((tiles, 32, TILE), jnp.bfloat16),
            pltpu.VMEM((half, 8, TILE), jnp.float32),
            pltpu.VMEM((half, 8, TILE), jnp.float32),
            pltpu.VMEM((half, 8, TILE), jnp.float32),
            pltpu.VMEM((2, 3, width), jnp.float32),
            pltpu.SemaphoreType.DMA((2,)),
        ]
        + [pltpu.VMEM((TILE, 3 * TILE), jnp.float32)] * RING
        + [pltpu.VMEM((4, 2 * TILE, TILE), jnp.bfloat16)] * RING,
        compiler_params=pltpu.CompilerParams(vmem_limit_bytes=40 * 2**20),
        name="tiles",
    )(*args)


def per_device(
    coords, velocities, coupling, charges, types, type_sigma, type_eps, near_tiles, accept
):
    width = coords.shape[2]
    half = width // TILE
    atoms = charges.shape[0]
    listed = near_tiles.shape[1]
    pos = coords.reshape(3, half, TILE)
    moving = velocities.reshape(3, half, TILE)
    cpl = coupling.reshape(2, half, TILE)
    five = jnp.concatenate([pos, cpl])
    other = swapped(five, "atom", 0)
    ten = jnp.concatenate([cpl, other[3:], pos, moving])
    pair1 = swapped(ten, "lam", 0)
    pair2 = swapped(ten, "lam", 1)

    look = lookup(charges, types, type_sigma, type_eps).reshape(3, 2 * half, TILE)
    first = lax.axis_index("atom") * half
    tiles = 2 * half
    local = jnp.mod(near_tiles.reshape(-1) - first + tiles, tiles)
    replica = lax.axis_index("lam")
    cycle = lax.axis_size("lam")
    odd = replica % 2
    flag1 = accept[replica - odd]
    flag2 = accept[jnp.mod(replica - 1 + odd + cycle, cycle)]
    near = jnp.concatenate([local, jnp.stack([first, flag1, flag2])]).astype(jnp.int32)

    energy, force, new_coords, new_velocities = call_kernel(
        (near, five, moving, other, pair1, pair2, look), half, listed
    )
    part = energy[:3, 0] * (0.5 / atoms)
    whole = part + swapped(part, "atom", 0)
    one, two = whole[1], whole[2]
    energies = jnp.stack([whole[0], jnp.where(odd == 1, one, two), jnp.where(odd == 1, two, one)])
    return (energies[None], force[None], new_coords[None], new_velocities[None])


def solution(mesh):
    in_specs = (
        P("lam", None, "atom"),
        P("lam", None, "atom"),
        P("lam", None, "atom"),
        P(),
        P(),
        P(),
        P(),
        P("atom", None),
        P(),
    )
    out_specs = (
        P("lam", None),
        P("lam", None, "atom"),
        P("lam", None, "atom"),
        P("lam", None, "atom"),
    )
    return jax.shard_map(
        per_device, mesh=mesh, in_specs=in_specs, out_specs=out_specs, check_vma=False
    )
```

time: 106 us -> 60.2 us (0.57)
  the two profiles are of different devices: /device:TPU:119 before, /device:TPU:8 now
where the time goes in v2:
time: 60.2 us; the launch traced here: 59.9 us
  Pallas kernels  30.3 us (50%)
  starting transfers between devices  12.1 us (20%)
  local copies, waits for them, and re-layouts  6.36 us (11%)
  waiting for transfers between devices  4.8 us (8%)
  between operations  3.3 us (5%)
  other arithmetic  2.7 us (4%)
    pallas_call x1, Pallas kernels, call_kernel(): pl.pallas_call(partial(tile_kernel, half=half, listed=listed), out_shape=...  30.3 us
    ppermute x4, starting transfers between devices, swapped(): return lax.ppermute(x, axis, pairs)  12.1 us
    unnamed x21, local copies, waits for them, and re-layouts  4.91 us
    ppermute x4, waiting for transfers between devices, swapped(): return lax.ppermute(x, axis, pairs)  4.8 us
    concatenate x1, other arithmetic, per_device(): jnp.concatenate([local, jnp.stack([first, flag1, flag2])]).astype(jnp.int32)  1.37 us
  transfers between devices with their start and end apart: 4, of which 3 were waited for; matrix products, arithmetic and copies ran while one was open for 7% of the time, Pallas kernels for 0%

profile of v2, /device:TPU:8, one launch (start us, length us, event | category | flops | bytes accessed | tf_op | source)
XLA Modules:
  0.0 59.9 jit_solution(2097878279299798530)
XLA Ops:
  0.6 0.0 copy-start.1
  0.6 0.9 %copy.25 = f32[1,2,64,128]{3,2,1,0:T(8,128)S(1)} copy(f32[1,2,64,128]{3,1,2,0:T(2,128)} %bitcast.37) | data formatting | bytes 131072
  1.5 0.0 copy-done.1
  1.6 2.2 %collective-permute-start = (f32[5,64,128]{2,1,0:T(8,128)S(1)}, f32[5,64,128]{2,1,0:T(8,128)S(1)}, u32[]{:S(2)}, u32[]{:S(2)}) collective-permute-start(f32[5,64,128]{2,1,0:T(8,128)S(1)} %pad_maximum_fusion.2.five_ref), channel_id=1, source_target_pairs={{0,1},{1,0},{2,3},{3,2},{4,5},{5,4},{6,7},{7,6},{8,9},{9,8},{10,11... | collective-permute-start | bytes 491528 | tf_op jit(solution)/shard_map/ppermute | solution.py:25
  3.8 0.0 copy-start.3
  3.8 0.7 %copy-done.3 = s32[64,5]{0,1:T(8,128)S(1)} copy-done((s32[64,5]{0,1:T(8,128)S(1)}, s32[64,5]{0,1:T(8,128)}, u32[]{:S(2)}) %copy-start.3) | copy-done | bytes 1304
  4.5 0.0 copy-start.5
  4.5 0.0 copy-start.6
  4.5 0.0 copy-start
  4.5 0.1 copy.16
  4.6 0.1 add.42
  4.8 0.4 copy-done.5
  5.2 0.0 copy-done.6
  5.2 2.4 %collective-permute-done.other_ref = f32[5,64,128]{2,1,0:T(8,128)S(1)} collective-permute-done((f32[5,64,128]{2,1,0:T(8,128)S(1)}, f32[5,64,128]{2,1,0:T(8,128)S(1)}, u32[]{:S(2)}, u32[]{:S(2)}) %collective-permute-start) | collective-permute-done | bytes 163872 | tf_op jit(solution)/shard_map/ppermute | solution.py:25
  7.6 0.0 copy-done
  7.6 0.0 copy-start.7
  7.7 8.5 %collective-permute-start.2 = (f32[10,64,128]{2,1,0:T(8,128)S(1)}, f32[10,64,128]{2,1,0:T(8,128)S(1)}, u32[]{:S(2)}, u32[]{:S(2)}) collective-permute-start(f32[10,64,128]{2,1,0:T(8,128)S(1)} %pad_maximum_fusion), channel_id=1, source_target_pairs={{2,4},{4,2},{6,8},{8,6},{10,12},{12,10},{14,16},{16,14},{18,20},{2... | collective-permute-start | bytes 983048 | tf_op jit(solution)/shard_map/ppermute | solution.py:25
  16.1 0.0 collective-permute-start.1
  16.1 0.0 copy-done.7
  16.1 0.4 convolution_bitcast_fusion
  16.5 0.0 copy-start.2
  16.6 0.0 copy-start.4
  16.6 0.6 %copy-done.4 = s32[128]{0:T(128)S(1)} copy-done((s32[128]{0:T(128)S(1)}, s32[128]{0:T(128)}, u32[]{:S(2)}) %copy-start.4) | copy-done | bytes 536
  17.2 0.6 fusion.7
  17.8 1.4 %pad_add_fusion.near_ref = s32[323]{0:T(512)S(1)} fusion(s32[1]{0:T(128)} %get-tuple-element.24, s32[1]{0:T(128)} %get-tuple-element.23, s32[1]{0:T(128)} %bitcast, s32[320]{0:T(512)S(1)} %add_select_fusion), kind=kLoop, calls=%fused_computation.13 | loop fusion | flops 969 | bytes 2584 | tf_op jit(solution)/shard_map/concatenate | solution.py:278
  19.2 0.0 copy-done.2
  19.2 1.7 %collective-permute-done.2.pair2_ref = f32[10,64,128]{2,1,0:T(8,128)S(1)} collective-permute-done((f32[10,64,128]{2,1,0:T(8,128)S(1)}, f32[10,64,128]{2,1,0:T(8,128)S(1)}, u32[]{:S(2)}, u32[]{:S(2)}) %collective-permute-start.2) | collective-permute-done | bytes 327712 | tf_op jit(solution)/shard_map/ppermute | solution.py:25
  20.9 0.0 collective-permute-done.1.pair1_ref
  20.9 30.3 %tiles.1 = (f32[8,128]{1,0:T(8,128)S(1)}, f32[3,8192]{1,0:T(4,128)S(1)}, f32[3,8192]{1,0:T(4,128)S(1)}, f32[3,8192]{1,0:T(4,128)S(1)}) custom-call(s32[323]{0:T(512)S(1)} %pad_add_fusion.near_ref, f32[5,64,128]{2,1,0:T(8,128)S(1)} %pad_maximum_fusion.2.five_ref, f32[3,64,128]{2,1,0:T(8,128)S(1)} %bitcast.28, ...), custom_call_target="tpu_custom_call" | custom-call | tf_op jit(solution)/shard_map/tiles/pallas_call | solution.py:226
  51.2 0.1 multiply_reduce_fusion
  51.3 0.7 %copy.17 = f32[1,3,8192]{2,0,1:T(1,128)} copy(f32[1,3,8192]{2,1,0:T(4,128)S(1)} %bitcast.31) | data formatting | bytes 196608
  52.0 1.4 %collective-permute-start.3 = (f32[3]{0:T(128)S(1)}, f32[3]{0:T(128)S(1)}, u32[]{:S(2)}, u32[]{:S(2)}) collective-permute-start(f32[3]{0:T(128)S(1)} %multiply_reduce_fusion), channel_id=1, source_target_pairs={{0,1},{1,0},{2,3},{3,2},{4,5},{5,4},{6,7},{7,6},{8,9},{9,8},{10,11... | collective-permute-start | bytes 44 | tf_op jit(solution)/shard_map/ppermute | solution.py:25
  53.4 0.7 %copy.18 = f32[1,3,8192]{2,0,1:T(1,128)} copy(f32[1,3,8192]{2,1,0:T(4,128)S(1)} %bitcast.30) | data formatting | bytes 196608
  54.1 0.7 %copy.19 = f32[1,3,8192]{2,0,1:T(1,128)} copy(f32[1,3,8192]{2,1,0:T(4,128)S(1)} %bitcast.29) | data formatting | bytes 196608
  54.9 0.7 %collective-permute-done.3 = f32[3]{0:T(128)S(1)} collective-permute-done((f32[3]{0:T(128)S(1)}, f32[3]{0:T(128)S(1)}, u32[]{:S(2)}, u32[]{:S(2)}) %collective-permute-start.3) | collective-permute-done | bytes 44 | tf_op jit(solution)/shard_map/ppermute | solution.py:25
  55.6 0.6 %fusion.6 = (f32[1]{0:T(128)}, f32[1]{0:T(128)}, f32[1]{0:T(128)}) fusion(f32[3]{0:T(128)S(1)} %add.51), kind=kLoop, calls=%fused_computation.22 | loop fusion | bytes 24 | tf_op jit(solution)/shard_map/slice | solution.py:286
  58.8 1.1 %maximum_bitcast_fusion = f32[1,3]{1,0:T(1,128)} fusion(f32[1]{0:T(128)} %bitcast.9, f32[1]{0:T(128)} %bitcast.8, f32[1]{0:T(128)} %get-tuple-element.20), kind=kLoop, calls=%fused_computation.18 | loop fusion | flops 6 | bytes 24 | tf_op jit(solution)/shard_map/broadcast_in_dim | solution.py:287
  (9 shorter events, 0.1 us)
Async XLA Ops:
  0.6 0.9 %copy-start.1 = (f32[1,3,8192]{2,0,1:T(1,128)S(1)}, f32[1,3,8192]{2,0,1:T(1,128)}, u32[]{:S(2)}) copy-start(f32[1,3,8192]{2,0,1:T(1,128)} %param.9) | copy-start | bytes 294916
  1.6 6.0 %collective-permute-start = (f32[5,64,128]{2,1,0:T(8,128)S(1)}, f32[5,64,128]{2,1,0:T(8,128)S(1)}, u32[]{:S(2)}, u32[]{:S(2)}) collective-permute-start(f32[5,64,128]{2,1,0:T(8,128)S(1)} %pad_maximum_fusion.2.five_ref), channel_id=1, source_target_pairs={{0,1},{1,0},{2,3},{3,2},{4,5},{5,4},{6,7},{7,6},{8,9},{9,8},{10,11... | collective-permute-start | bytes 491528 | tf_op jit(solution)/shard_map/ppermute | solution.py:25
  3.8 0.7 %copy-start.3 = (s32[64,5]{0,1:T(8,128)S(1)}, s32[64,5]{0,1:T(8,128)}, u32[]{:S(2)}) copy-start(s32[64,5]{0,1:T(8,128)} %param.16) | copy-start | bytes 3844
  4.5 0.7 %copy-start.5 = (f32[16]{0:T(128)S(1)}, f32[16]{0:T(128)}, u32[]{:S(2)}) copy-start(f32[16]{0:T(128)} %param.14) | copy-start | bytes 196
  4.5 0.7 %copy-start.6 = (f32[16]{0:T(128)S(1)}, f32[16]{0:T(128)}, u32[]{:S(2)}) copy-start(f32[16]{0:T(128)} %param.15) | copy-start | bytes 196
  4.5 3.1 %copy-start = (f32[1,3,8192]{2,0,1:T(1,128)S(1)}, f32[1,3,8192]{2,0,1:T(1,128)}, u32[]{:S(2)}) copy-start(f32[1,3,8192]{2,0,1:T(1,128)} %param.10) | copy-start | bytes 294916
  7.6 8.5 %copy-start.7 = (s32[16384]{0:T(1024)S(1)}, s32[16384]{0:T(1024)}, u32[]{:S(2)}) copy-start(s32[16384]{0:T(1024)} %param.13) | copy-start | bytes 196612
  7.7 13.2 %collective-permute-start.2 = (f32[10,64,128]{2,1,0:T(8,128)S(1)}, f32[10,64,128]{2,1,0:T(8,128)S(1)}, u32[]{:S(2)}, u32[]{:S(2)}) collective-permute-start(f32[10,64,128]{2,1,0:T(8,128)S(1)} %pad_maximum_fusion), channel_id=1, source_target_pairs={{2,4},{4,2},{6,8},{8,6},{10,12},{12,10},{14,16},{16,14},{18,20},{2... | collective-permute-start | bytes 983048 | tf_op jit(solution)/shard_map/ppermute | solution.py:25
  16.1 4.8 %collective-permute-start.1 = (f32[10,64,128]{2,1,0:T(8,128)S(1)}, f32[10,64,128]{2,1,0:T(8,128)S(1)}, u32[]{:S(2)}, u32[]{:S(2)}) collective-permute-start(f32[10,64,128]{2,1,0:T(8,128)S(1)} %pad_maximum_fusion), channel_id=1, source_target_pairs={{0,2},{2,0},{4,6},{6,4},{8,10},{10,8},{12,14},{14,12},{16,18},{18,... | collective-permute-start | bytes 983048 | tf_op jit(solution)/shard_map/ppermute | solution.py:25
  16.5 2.7 %copy-start.2 = (f32[16384]{0:T(1024)S(1)}, f32[16384]{0:T(1024)}, u32[]{:S(2)}) copy-start(f32[16384]{0:T(1024)} %param.12) | copy-start | bytes 196612
  16.6 0.7 %copy-start.4 = (s32[128]{0:T(128)S(1)}, s32[128]{0:T(128)}, u32[]{:S(2)}) copy-start(s32[128]{0:T(128)} %param.17) | copy-start | bytes 1540
  52.0 3.6 %collective-permute-start.3 = (f32[3]{0:T(128)S(1)}, f32[3]{0:T(128)S(1)}, u32[]{:S(2)}, u32[]{:S(2)}) collective-permute-start(f32[3]{0:T(128)S(1)} %multiply_reduce_fusion), channel_id=1, source_target_pairs={{0,1},{1,0},{2,3},{3,2},{4,5},{5,4},{6,7},{7,6},{8,9},{9,8},{10,11... | collective-permute-start | bytes 44 | tf_op jit(solution)/shard_map/ppermute | solution.py:25

commit v3 on v2

--- a/solution.py
+++ b/solution.py
@@ -13,7 +13,8 @@
 RING = 5
 AHEAD = 3
 LATE = 2
-ROWS = 4
+ROWS = 16
+PREP = 8
 
 
 def swapped(x, axis, first):
@@ -92,14 +93,6 @@
             )
             q1, q2, q3 = split3(sides)
             side_ref[dest] = jnp.concatenate([q1, q2, q1, q2, q3, q1], axis=0)
-            lanes = pl.ds(pl.multiple_of(t * TILE, TILE), TILE)
-            own_rows = [x, y, z] + rows(moving_ref, *range(3))
-            for n, (mine, one_row, two_row) in enumerate(
-                zip(own_rows, rows(pair1_ref, *range(4, 10)), rows(pair2_ref, *range(4, 10)))
-            ):
-                new_ref[n // 3, pl.ds(n % 3, 1), lanes] = jnp.where(
-                    take1, one_row, jnp.where(take2, two_row, mine)
-                )
 
     def prep_own(t, _):
         prepare(t, five_ref, 0, True)
@@ -109,14 +102,19 @@
         prepare(t, other_ref, 2, False)
         return 0
 
-    lax.fori_loop(0, half, prep_own, 0)
+    for j in range(6):
+        mine = five_ref[j] if j < 3 else moving_ref[j - 3]
+        new_ref[j // 3, j % 3] = jnp.where(
+            take1, pair1_ref[4 + j], jnp.where(take2, pair2_ref[4 + j], mine)
+        )
     copies = [
         pltpu.make_async_copy(new_ref.at[n], out, sem.at[n])
         for n, out in enumerate((coords_out, moving_out))
     ]
     for copy in copies:
         copy.start()
-    lax.fori_loop(0, half, prep_other, 0)
+    lax.fori_loop(0, half, prep_own, 0, unroll=PREP)
+    lax.fori_loop(0, half, prep_other, 0, unroll=PREP)
 
     def distances(i, k):
         c = near_ref[i * listed + k]
@@ -162,11 +160,12 @@
         zc = zc_ref[i]
         ze = ze_ref[i]
         own = own_times.astype(jnp.float32) * (DELTA_SOFT**-0.5)
-        lanes = pl.ds(pl.multiple_of(i * TILE, TILE), TILE)
         pos = pos_ref[i, 0:3]
-        force_ref[:, lanes] = zc[0:1] * (pos * sum_i[0:1] - sum_i[3:6]) + 48.0 * ze[0:1] * (
+        force = zc[0:1] * (pos * sum_i[0:1] - sum_i[3:6]) + 48.0 * ze[0:1] * (
             pos * sum_f[0:1] - sum_f[3:6]
         )
+        for j in range(3):
+            force_ref[j, pl.ds(i, 1), :] = force[j : j + 1]
         return total + zc * (sum_a - own * zc) + 4.0 * (ze * sum_b)
 
     def nothing():
@@ -205,7 +204,12 @@
     for k in range(listed - LATE, listed):
         acc = gather(half - 1, k, acc)
     total = finish(half - 1, acc, total)
-    energy_ref[...] = jnp.broadcast_to(jnp.sum(total, axis=1, keepdims=True), (8, TILE))
+    sums = jnp.sum(total, axis=1, keepdims=True) * (0.5 / (2 * half * TILE))
+    is_odd = near_ref[half * listed + 3] == 1
+    lower = jnp.where(is_odd, sums[1:2], sums[2:3])
+    upper = jnp.where(is_odd, sums[2:3], sums[1:2])
+    lane = lax.broadcasted_iota(jnp.int32, (1, TILE), 1)
+    energy_ref[...] = jnp.where(lane == 0, sums[0:1], jnp.where(lane == 1, lower, upper))
     for copy in copies:
         copy.wait()
 
@@ -219,17 +223,16 @@
 
 
 def call_kernel(args, half, listed):
-    width = half * TILE
     tiles = 2 * half
     vmem = pl.BlockSpec(memory_space=pltpu.VMEM)
     hbm = pl.BlockSpec(memory_space=pltpu.HBM)
     return pl.pallas_call(
         partial(tile_kernel, half=half, listed=listed),
         out_shape=(
-            jax.ShapeDtypeStruct((8, TILE), jnp.float32),
-            jax.ShapeDtypeStruct((3, width), jnp.float32),
-            jax.ShapeDtypeStruct((3, width), jnp.float32),
-            jax.ShapeDtypeStruct((3, width), jnp.float32),
+            jax.ShapeDtypeStruct((1, TILE), jnp.float32),
+            jax.ShapeDtypeStruct((3, half, TILE), jnp.float32),
+            jax.ShapeDtypeStruct((3, half, TILE), jnp.float32),
+            jax.ShapeDtypeStruct((3, half, TILE), jnp.float32),
         ),
         in_specs=[pl.BlockSpec(memory_space=pltpu.SMEM)] + [vmem] * 6,
         out_specs=(vmem, vmem, hbm, hbm),
@@ -240,7 +243,7 @@
             pltpu.VMEM((half, 8, TILE), jnp.float32),
             pltpu.VMEM((half, 8, TILE), jnp.float32),
             pltpu.VMEM((half, 8, TILE), jnp.float32),
-            pltpu.VMEM((2, 3, width), jnp.float32),
+            pltpu.VMEM((2, 3, half, TILE), jnp.float32),
             pltpu.SemaphoreType.DMA((2,)),
         ]
         + [pltpu.VMEM((TILE, 3 * TILE), jnp.float32)] * RING
@@ -255,17 +258,12 @@
 ):
     width = coords.shape[2]
     half = width // TILE
-    atoms = charges.shape[0]
     listed = near_tiles.shape[1]
     pos = coords.reshape(3, half, TILE)
     moving = velocities.reshape(3, half, TILE)
     cpl = coupling.reshape(2, half, TILE)
     five = jnp.concatenate([pos, cpl])
     other = swapped(five, "atom", 0)
-    ten = jnp.concatenate([cpl, other[3:], pos, moving])
-    pair1 = swapped(ten, "lam", 0)
-    pair2 = swapped(ten, "lam", 1)
-
     look = lookup(charges, types, type_sigma, type_eps).reshape(3, 2 * half, TILE)
     first = lax.axis_index("atom") * half
     tiles = 2 * half
@@ -275,16 +273,24 @@
     odd = replica % 2
     flag1 = accept[replica - odd]
     flag2 = accept[jnp.mod(replica - 1 + odd + cycle, cycle)]
-    near = jnp.concatenate([local, jnp.stack([first, flag1, flag2])]).astype(jnp.int32)
+    near = jnp.concatenate([local, jnp.stack([first, flag1, flag2, odd])]).astype(jnp.int32)
+
+    other, look, near = lax.optimization_barrier((other, look, near))
+    ten = jnp.concatenate([cpl, other[3:], pos, moving])
+    pair1 = swapped(ten, "lam", 0)
+    pair2 = swapped(ten, "lam", 1)
 
     energy, force, new_coords, new_velocities = call_kernel(
         (near, five, moving, other, pair1, pair2, look), half, listed
     )
-    part = energy[:3, 0] * (0.5 / atoms)
-    whole = part + swapped(part, "atom", 0)
-    one, two = whole[1], whole[2]
-    energies = jnp.stack([whole[0], jnp.where(odd == 1, one, two), jnp.where(odd == 1, two, one)])
-    return (energies[None], force[None], new_coords[None], new_velocities[None])
+    part = energy[:, :3]
+    shape = coords.shape
+    return (
+        part + swapped(part, "atom", 0),
+        force.reshape(shape),
+        new_coords.reshape(shape),
+        new_velocities.reshape(shape),
+    )
 
 
 def solution(mesh):

time: 60.2 us -> 51.9 us (0.86)
  Pallas kernels: 30.3 us -> 26.2 us
  between operations: 3.3 us -> 0.81 us
  other arithmetic: 2.7 us -> 0.58 us
  waiting for transfers between devices: 4.8 us -> 6.57 us
  local copies, waits for them, and re-layouts: 6.36 us -> 5.26 us
    pallas_call x1, Pallas kernels: 30.3 us -> 26.2 us  [call_kernel(): pl.pallas_call(partial(tile_kernel, half=half, listed=listed), out_shape=...]
    unnamed x21 -> x18, local copies, waits for them, and re-layouts: 4.91 us -> 3.06 us
    ppermute x4, waiting for transfers between devices: 4.8 us -> 6.57 us  [swapped(): return lax.ppermute(x, axis, pairs)]
    concatenate x0 -> x1, local copies, waits for them, and re-layouts: none -> 1.37 us  [per_device(): jnp.concatenate([local, jnp.stack([first, flag1, flag2, odd])])]
    concatenate x1 -> x0, other arithmetic: 1.37 us -> none  [per_device(): jnp.concatenate([local, jnp.stack([first, flag1, flag2])]).astype(jnp.int32)]
    broadcast_in_dim x1 -> x0, other arithmetic: 1.15 us -> none  [per_device(): return (energies[None], force[None], new_coords[None], new_velocities[None])]
    slice x1 -> x0, local copies, waits for them, and re-layouts: 0.62 us -> none  [per_device(): whole[0]]
  transfers between devices with their start and end apart: 4 -> 4, of which waited for: 3 -> 2; matrix products, arithmetic and copies ran while one was open for 7% -> 5% of each run, Pallas kernels for 0% -> 0%
where the time goes in v3:
time: 51.9 us; the launch traced here: 51.6 us
  Pallas kernels  26.2 us (50%)
  starting transfers between devices  11.8 us (23%)
  waiting for transfers between devices  6.57 us (13%)
  local copies, waits for them, and re-layouts  5.26 us (10%)
  between operations  0.81 us (2%)
  other arithmetic  0.58 us (1%)
    pallas_call x1, Pallas kernels, call_kernel(): pl.pallas_call(partial(tile_kernel, half=half, listed=listed), out_shape=...  26.2 us
    ppermute x4, starting transfers between devices, swapped(): return lax.ppermute(x, axis, pairs)  11.8 us
    ppermute x4, waiting for transfers between devices, swapped(): return lax.ppermute(x, axis, pairs)  6.57 us
    unnamed x18, local copies, waits for them, and re-layouts  3.06 us
    concatenate x1, local copies, waits for them, and re-layouts, per_device(): jnp.concatenate([local, jnp.stack([first, flag1, flag2, odd])])  1.37 us
  transfers between devices with their start and end apart: 4, of which 2 were waited for; matrix products, arithmetic and copies ran while one was open for 5% of the time, Pallas kernels for 0%

profile of v3, /device:TPU:8, one launch (start us, length us, event | category | flops | bytes accessed | tf_op | source)
XLA Modules:
  0.0 51.6 jit_solution(7393654661570708060)
XLA Ops:
  0.6 0.0 copy-start.1
  0.6 0.9 %copy.25 = f32[1,2,64,128]{3,2,1,0:T(8,128)S(1)} copy(f32[1,2,64,128]{3,1,2,0:T(2,128)} %bitcast.31) | data formatting | bytes 131072
  1.5 0.0 copy-done.1
  1.6 0.0 copy-start.3
  1.6 0.0 copy-start.7
  1.6 2.2 %collective-permute-start = (f32[5,64,128]{2,1,0:T(8,128)S(1)}, f32[5,64,128]{2,1,0:T(8,128)S(1)}, u32[]{:S(2)}, u32[]{:S(2)}) collective-permute-start(f32[5,64,128]{2,1,0:T(8,128)S(1)} %pad_maximum_fusion.2.five_ref), channel_id=1, source_target_pairs={{0,1},{1,0},{2,3},{3,2},{4,5},{5,4},{6,7},{7,6},{8,9},{9,8},{10,11... | collective-permute-start | bytes 491528 | tf_op jit(solution)/shard_map/ppermute | solution.py:26
  3.8 0.0 copy-done.3
  3.8 0.1 copy.16
  3.9 0.1 add.42
  4.1 0.0 copy-start.5
  4.1 0.0 copy-start.6
  4.1 0.6 %copy-done.5 = f32[16]{0:T(128)S(1)} copy-done((f32[16]{0:T(128)S(1)}, f32[16]{0:T(128)}, u32[]{:S(2)}) %copy-start.5) | copy-done | bytes 88
  4.7 0.0 copy-done.6
  4.8 0.0 copy-done.7
  4.8 0.4 convolution_bitcast_fusion
  5.2 0.0 copy-start.4
  5.2 0.0 copy-start.2
  5.3 0.6 %copy-done.4 = s32[128]{0:T(128)S(1)} copy-done((s32[128]{0:T(128)S(1)}, s32[128]{0:T(128)}, u32[]{:S(2)}) %copy-start.4) | copy-done | bytes 536
  5.9 0.6 %fusion.6 = (s32[1]{0:T(128)}, s32[1]{0:T(128)}) fusion(s32[128]{0:T(128)S(1)} %copy-done.4, s32[]{:T(128)S(6)} %select_n.27, s32[]{:T(128)S(6)} %select_n.25), kind=kLoop, calls=%fused_computation.20 | loop fusion | bytes 24 | tf_op jit(solution)/shard_map/dynamic_slice | solution.py:275
  6.5 1.4 %concatenate.21.near_ref = s32[324]{0:T(512)S(1)} concatenate(s32[320]{0:T(512)S(1)} %add_select_fusion, s32[1]{0:T(128)} %bitcast.4, s32[1]{0:T(128)} %get-tuple-element.27, s32[1]{0:T(128)} %get-tuple-element.26, s32[1]{0:T(128)} %bitcast.5), dimensions={0} | concatenate | bytes 2592 | tf_op jit(solution)/shard_map/concatenate | solution.py:276
  7.8 0.0 copy-done.2
  7.9 0.0 copy-start
  7.9 0.0 collective-permute-done.other_ref
  7.9 0.9 %copy-done = f32[1,3,8192]{2,0,1:T(1,128)S(1)} copy-done((f32[1,3,8192]{2,0,1:T(1,128)S(1)}, f32[1,3,8192]{2,0,1:T(1,128)}, u32[]{:S(2)}) %copy-start) | copy-done | bytes 98328
  8.8 7.7 %collective-permute-start.2 = (f32[10,64,128]{2,1,0:T(8,128)S(1)}, f32[10,64,128]{2,1,0:T(8,128)S(1)}, u32[]{:S(2)}, u32[]{:S(2)}) collective-permute-start(f32[10,64,128]{2,1,0:T(8,128)S(1)} %pad_maximum_fusion), channel_id=1, source_target_pairs={{2,4},{4,2},{6,8},{8,6},{10,12},{12,10},{14,16},{16,14},{18,20},{2... | collective-permute-start | bytes 983048 | tf_op jit(solution)/shard_map/ppermute | solution.py:26
  16.5 0.0 collective-permute-start.1
  16.5 4.8 %collective-permute-done.2.pair2_ref = f32[10,64,128]{2,1,0:T(8,128)S(1)} collective-permute-done((f32[10,64,128]{2,1,0:T(8,128)S(1)}, f32[10,64,128]{2,1,0:T(8,128)S(1)}, u32[]{:S(2)}, u32[]{:S(2)}) %collective-permute-start.2) | collective-permute-done | bytes 327712 | tf_op jit(solution)/shard_map/ppermute | solution.py:26
  21.3 0.0 collective-permute-done.1.pair1_ref
  21.3 26.2 %tiles.1 = (f32[1,128]{1,0:T(1,128)S(1)}, f32[3,64,128]{2,1,0:T(8,128)}, f32[3,64,128]{2,1,0:T(8,128)}, f32[3,64,128]{2,1,0:T(8,128)}) custom-call(s32[324]{0:T(512)S(1)} %concatenate.21.near_ref, f32[5,64,128]{2,1,0:T(8,128)S(1)} %pad_maximum_fusion.2.five_ref, f32[3,64,128]{2,1,0:T(8,128)S(1)} %bitcast.24, ...), custom_call_target="tpu_custom_call" | custom-call | tf_op jit(solution)/shard_map/tiles/pallas_call | solution.py:229
  47.5 1.8 %collective-permute-start.3 = (f32[1,3]{1,0:T(1,128)S(1)}, f32[1,3]{1,0:T(1,128)S(1)}, u32[]{:S(2)}, u32[]{:S(2)}) collective-permute-start(f32[1,3]{1,0:T(1,128)S(1)} %bitcast.25), channel_id=1, source_target_pairs={{0,1},{1,0},{2,3},{3,2},{4,5},{5,4},{6,7},{7,6},{8,9},{9,8},{10,11... | collective-permute-start | bytes 44 | tf_op jit(solution)/shard_map/ppermute | solution.py:26
  49.3 1.8 %collective-permute-done.3 = f32[1,3]{1,0:T(1,128)S(1)} collective-permute-done((f32[1,3]{1,0:T(1,128)S(1)}, f32[1,3]{1,0:T(1,128)S(1)}, u32[]{:S(2)}, u32[]{:S(2)}) %collective-permute-start.3) | collective-permute-done | bytes 44 | tf_op jit(solution)/shard_map/ppermute | solution.py:26
  51.1 0.5 slice_add_fusion
  (8 shorter events, 0.1 us)
Async XLA Ops:
  0.6 0.9 %copy-start.1 = (f32[1,3,8192]{2,0,1:T(1,128)S(1)}, f32[1,3,8192]{2,0,1:T(1,128)}, u32[]{:S(2)}) copy-start(f32[1,3,8192]{2,0,1:T(1,128)} %param.9) | copy-start | bytes 294916
  1.6 2.3 %copy-start.3 = (s32[64,5]{0,1:T(8,128)S(1)}, s32[64,5]{0,1:T(8,128)}, u32[]{:S(2)}) copy-start(s32[64,5]{0,1:T(8,128)} %param.16) | copy-start | bytes 3844
  1.6 3.2 %copy-start.7 = (s32[16384]{0:T(1024)S(1)}, s32[16384]{0:T(1024)}, u32[]{:S(2)}) copy-start(s32[16384]{0:T(1024)} %param.13) | copy-start | bytes 196612
  1.6 6.3 %collective-permute-start = (f32[5,64,128]{2,1,0:T(8,128)S(1)}, f32[5,64,128]{2,1,0:T(8,128)S(1)}, u32[]{:S(2)}, u32[]{:S(2)}) collective-permute-start(f32[5,64,128]{2,1,0:T(8,128)S(1)} %pad_maximum_fusion.2.five_ref), channel_id=1, source_target_pairs={{0,1},{1,0},{2,3},{3,2},{4,5},{5,4},{6,7},{7,6},{8,9},{9,8},{10,11... | collective-permute-start | bytes 491528 | tf_op jit(solution)/shard_map/ppermute | solution.py:26
  4.1 0.7 %copy-start.5 = (f32[16]{0:T(128)S(1)}, f32[16]{0:T(128)}, u32[]{:S(2)}) copy-start(f32[16]{0:T(128)} %param.14) | copy-start | bytes 196
  4.1 0.7 %copy-start.6 = (f32[16]{0:T(128)S(1)}, f32[16]{0:T(128)}, u32[]{:S(2)}) copy-start(f32[16]{0:T(128)} %param.15) | copy-start | bytes 196
  5.2 0.7 %copy-start.4 = (s32[128]{0:T(128)S(1)}, s32[128]{0:T(128)}, u32[]{:S(2)}) copy-start(s32[128]{0:T(128)} %param.17) | copy-start | bytes 1540
  5.2 2.6 %copy-start.2 = (f32[16384]{0:T(1024)S(1)}, f32[16384]{0:T(1024)}, u32[]{:S(2)}) copy-start(f32[16384]{0:T(1024)} %param.12) | copy-start | bytes 196612
  7.9 0.9 %copy-start = (f32[1,3,8192]{2,0,1:T(1,128)S(1)}, f32[1,3,8192]{2,0,1:T(1,128)}, u32[]{:S(2)}) copy-start(f32[1,3,8192]{2,0,1:T(1,128)} %param.10) | copy-start | bytes 294916
  8.8 12.5 %collective-permute-start.2 = (f32[10,64,128]{2,1,0:T(8,128)S(1)}, f32[10,64,128]{2,1,0:T(8,128)S(1)}, u32[]{:S(2)}, u32[]{:S(2)}) collective-permute-start(f32[10,64,128]{2,1,0:T(8,128)S(1)} %pad_maximum_fusion), channel_id=1, source_target_pairs={{2,4},{4,2},{6,8},{8,6},{10,12},{12,10},{14,16},{16,14},{18,20},{2... | collective-permute-start | bytes 983048 | tf_op jit(solution)/shard_map/ppermute | solution.py:26
  16.5 4.8 %collective-permute-start.1 = (f32[10,64,128]{2,1,0:T(8,128)S(1)}, f32[10,64,128]{2,1,0:T(8,128)S(1)}, u32[]{:S(2)}, u32[]{:S(2)}) collective-permute-start(f32[10,64,128]{2,1,0:T(8,128)S(1)} %pad_maximum_fusion), channel_id=1, source_target_pairs={{0,2},{2,0},{4,6},{6,4},{8,10},{10,8},{12,14},{14,12},{16,18},{18,... | collective-permute-start | bytes 983048 | tf_op jit(solution)/shard_map/ppermute | solution.py:26
  47.5 3.7 %collective-permute-start.3 = (f32[1,3]{1,0:T(1,128)S(1)}, f32[1,3]{1,0:T(1,128)S(1)}, u32[]{:S(2)}, u32[]{:S(2)}) collective-permute-start(f32[1,3]{1,0:T(1,128)S(1)} %bitcast.25), channel_id=1, source_target_pairs={{0,1},{1,0},{2,3},{3,2},{4,5},{5,4},{6,7},{7,6},{8,9},{9,8},{10,11... | collective-permute-start | bytes 44 | tf_op jit(solution)/shard_map/ppermute | solution.py:26

commit v4 on v3

--- a/solution.py
+++ b/solution.py
@@ -40,28 +40,16 @@
     return one, two
 
 
-def tile_kernel(
-    near_ref,
-    five_ref, moving_ref, other_ref, pair1_ref, pair2_ref, look_ref,
-    energy_ref, force_ref, coords_out, moving_out,
-    feat_ref, side_ref, vec_ref, zc_ref, ze_ref, pos_ref, new_ref, sem, *work_refs,
-    half, listed,
+def place_kernel(
+    info_ref, own_ref, other_ref, look_ref, feat_ref, side_ref, pos_ref, *, half
 ):
-    first = near_ref[half * listed]
-    take1 = near_ref[half * listed + 1] == 1
-    take2 = near_ref[half * listed + 2] == 1
-    dist_refs, mat_refs = work_refs[:RING], work_refs[RING:]
-
-    def prepare(t, from_ref, at, own):
-        def rows(ref, *js):
-            return [ref[j, pl.ds(t, 1), :] for j in js]
-
+    first = info_ref[0]
+
+    def prepare(t, from_ref, own):
         there = t + (first if own else half - first)
         dest = t if own else t + half
-        charge0, depth0, h = [look_ref[j, pl.ds(there, 1), :] for j in range(3)]
-        x, y, z, cpl0, cpl1 = rows(from_ref, *range(5))
-        low0, low1 = rows(pair1_ref, at, at + 1)
-        up0, up1 = rows(pair2_ref, at, at + 1)
+        h = look_ref[2, pl.ds(there, 1), :]
+        x, y, z = [from_ref[j, pl.ds(t, 1), :] for j in range(2, 5)]
         n = x * x + y * y + z * z
         h2 = h * h
         one = jnp.ones_like(n)
@@ -69,19 +57,9 @@
         feats = jnp.concatenate([x, y, z, n, h, h2, one, zero], axis=0)
         p1, p2, p3 = split3(feats)
         feat_ref[dest] = jnp.concatenate([p1, p1, p2, p2, p1, p3], axis=0)
-        c0 = charge0 * cpl0
-        e0 = depth0 * cpl1
-        pos = feats[0:3]
-        zc = jnp.concatenate([c0, charge0 * low0, charge0 * up0, c0 * pos, zero, zero], axis=0)
-        ze = jnp.concatenate([e0, depth0 * low1, depth0 * up1, e0 * pos, zero, zero], axis=0)
-        c1, c2 = split2(zc)
-        e1, e2 = split2(ze)
-        vec_ref[dest] = jnp.concatenate([c1, c2, e1, e2], axis=0)
         if own:
-            zc_ref[dest] = zc
-            ze_ref[dest] = ze
             pos_ref[dest] = feats
-            m = -2.0 * pos
+            m = -2.0 * feats[0:3]
             hh = 2.0 * h
             sides = jnp.concatenate(
                 [
@@ -95,17 +73,74 @@
             side_ref[dest] = jnp.concatenate([q1, q2, q1, q2, q3, q1], axis=0)
 
     def prep_own(t, _):
-        prepare(t, five_ref, 0, True)
+        prepare(t, own_ref, True)
         return 0
 
     def prep_other(t, _):
-        prepare(t, other_ref, 2, False)
+        prepare(t, other_ref, False)
         return 0
 
+    lax.fori_loop(0, half, prep_own, 0, unroll=PREP)
+    lax.fori_loop(0, half, prep_other, 0, unroll=PREP)
+
+
+def tile_kernel(
+    near_ref, info_ref,
+    own_ref, other_ref, pair1_ref, pair2_ref, far_ref, look_ref, feat_ref, side_ref, pos_ref,
+    energy_ref, force_ref, coords_out, moving_out,
+    vec_ref, zc_ref, ze_ref, new_ref, sem, *work_refs,
+    half, listed,
+):
+    first = info_ref[0]
+    take1 = info_ref[1] == 1
+    take2 = info_ref[2] == 1
+    dist_refs, mat_refs = work_refs[:RING], work_refs[RING:]
+
+    def listed_tile(i, k):
+        c = near_ref[i, k] - first
+        return jnp.where(c < 0, c + 2 * half, c)
+
+    def prepare(t, own):
+        from_ref = own_ref if own else other_ref
+        there = t + (first if own else half - first)
+        dest = t if own else t + half
+
+        def row(ref, j):
+            return ref[j, pl.ds(t, 1), :]
+
+        charge0, depth0 = [look_ref[j, pl.ds(there, 1), :] for j in range(2)]
+        cpl0, cpl1, x, y, z = [row(from_ref, j) for j in range(5)]
+        if own:
+            one0, one1, two0, two1 = [row(r, j) for r in (pair1_ref, pair2_ref) for j in range(2)]
+        else:
+            one0, one1, two0, two1 = [row(far_ref, j) for j in range(4)]
+        zero = jnp.zeros_like(x)
+        c0 = charge0 * cpl0
+        e0 = depth0 * cpl1
+        zc = jnp.concatenate(
+            [c0, charge0 * one0, charge0 * two0, c0 * x, c0 * y, c0 * z, zero, zero], axis=0
+        )
+        ze = jnp.concatenate(
+            [e0, depth0 * one1, depth0 * two1, e0 * x, e0 * y, e0 * z, zero, zero], axis=0
+        )
+        c1, c2 = split2(zc)
+        e1, e2 = split2(ze)
+        vec_ref[dest] = jnp.concatenate([c1, c2, e1, e2], axis=0)
+        if own:
+            zc_ref[dest] = zc
+            ze_ref[dest] = ze
+
+    def prep_own(t, _):
+        prepare(t, True)
+        return 0
+
+    def prep_other(t, _):
+        prepare(t, False)
+        return 0
+
     for j in range(6):
-        mine = five_ref[j] if j < 3 else moving_ref[j - 3]
         new_ref[j // 3, j % 3] = jnp.where(
-            take1, pair1_ref[4 + j], jnp.where(take2, pair2_ref[4 + j], mine)
+            take1, pair1_ref[2 + j], jnp.where(take2, pair2_ref[2 + j], own_ref[2 + j])
         )
     copies = [
         pltpu.make_async_copy(new_ref.at[n], out, sem.at[n])
@@ -117,7 +152,7 @@
     lax.fori_loop(0, half, prep_other, 0, unroll=PREP)
 
     def distances(i, k):
-        c = near_ref[i * listed + k]
+        c = listed_tile(i, k)
         dist_refs[k % RING][...] = lax.dot_general(
             feat_ref[c], side_ref[i], (((0,), (0,)), ((), ())),
             preferred_element_type=jnp.float32,
@@ -143,7 +178,7 @@
                 mat_ref[n, low_rows] = lo
 
     def gather(i, k, acc):
-        vec = vec_ref[near_ref[i * listed + k]]
+        vec = vec_ref[listed_tile(i, k)]
         cc = jnp.concatenate([vec[:16], vec[:16]], axis=1)
         ee = jnp.concatenate([vec[16:], vec[16:]], axis=1)
         mat_ref = mat_refs[k % RING]
@@ -156,7 +191,7 @@
         sum_a, sum_b, sum_i, sum_f = [a[:8] + a[8:] for a in acc]
         own_times = jnp.int32(0)
         for k in range(listed):
-            own_times = own_times + jnp.where(near_ref[i * listed + k] == i, 1, 0)
+            own_times = own_times + jnp.where(listed_tile(i, k) == i, 1, 0)
         zc = zc_ref[i]
         ze = ze_ref[i]
         own = own_times.astype(jnp.float32) * (DELTA_SOFT**-0.5)
@@ -205,7 +240,7 @@
         acc = gather(half - 1, k, acc)
     total = finish(half - 1, acc, total)
     sums = jnp.sum(total, axis=1, keepdims=True) * (0.5 / (2 * half * TILE))
-    is_odd = near_ref[half * listed + 3] == 1
+    is_odd = info_ref[3] == 1
     lower = jnp.where(is_odd, sums[1:2], sums[2:3])
     upper = jnp.where(is_odd, sums[2:3], sums[1:2])
     lane = lax.broadcasted_iota(jnp.int32, (1, TILE), 1)
@@ -222,10 +257,25 @@
     return jnp.concatenate([charges[None], looked])
 
 
-def call_kernel(args, half, listed):
+def call_kernels(near, info, own, other, pair1, pair2, far, look):
+    half, listed = near.shape
     tiles = 2 * half
     vmem = pl.BlockSpec(memory_space=pltpu.VMEM)
+    smem = pl.BlockSpec(memory_space=pltpu.SMEM)
     hbm = pl.BlockSpec(memory_space=pltpu.HBM)
+    limit = pltpu.CompilerParams(vmem_limit_bytes=40 * 2**20)
+    feat, side, pos = pl.pallas_call(
+        partial(place_kernel, half=half),
+        out_shape=(
+            jax.ShapeDtypeStruct((tiles, 48, TILE), jnp.bfloat16),
+            jax.ShapeDtypeStruct((half, 48, 3 * TILE), jnp.bfloat16),
+            jax.ShapeDtypeStruct((half, 8, TILE), jnp.float32),
+        ),
+        in_specs=[smem, vmem, vmem, vmem],
+        out_specs=(vmem, vmem, vmem),
+        compiler_params=limit,
+        name="places",
+    )(info, own, other, look)
     return pl.pallas_call(
         partial(tile_kernel, half=half, listed=listed),
         out_shape=(
@@ -234,13 +284,10 @@
             jax.ShapeDtypeStruct((3, half, TILE), jnp.float32),
             jax.ShapeDtypeStruct((3, half, TILE), jnp.float32),
         ),
-        in_specs=[pl.BlockSpec(memory_space=pltpu.SMEM)] + [vmem] * 6,
+        in_specs=[smem, smem] + [vmem] * 9,
         out_specs=(vmem, vmem, hbm, hbm),
         scratch_shapes=[
-            pltpu.VMEM((tiles, 48, TILE), jnp.bfloat16),
-            pltpu.VMEM((half, 48, 3 * TILE), jnp.bfloat16),
             pltpu.VMEM((tiles, 32, TILE), jnp.bfloat16),
-            pltpu.VMEM((half, 8, TILE), jnp.float32),
             pltpu.VMEM((half, 8, TILE), jnp.float32),
             pltpu.VMEM((half, 8, TILE), jnp.float32),
             pltpu.VMEM((2, 3, half, TILE), jnp.float32),
@@ -248,40 +295,38 @@
         ]
         + [pltpu.VMEM((TILE, 3 * TILE), jnp.float32)] * RING
         + [pltpu.VMEM((4, 2 * TILE, TILE), jnp.bfloat16)] * RING,
-        compiler_params=pltpu.CompilerParams(vmem_limit_bytes=40 * 2**20),
+        compiler_params=limit,
         name="tiles",
-    )(*args)
+    )(near, info, own, other, pair1, pair2, far, look, feat, side, pos)
 
 
 def per_device(
     coords, velocities, coupling, charges, types, type_sigma, type_eps, near_tiles, accept
 ):
-    width = coords.shape[2]
-    half = width // TILE
-    listed = near_tiles.shape[1]
-    pos = coords.reshape(3, half, TILE)
-    moving = velocities.reshape(3, half, TILE)
-    cpl = coupling.reshape(2, half, TILE)
-    five = jnp.concatenate([pos, cpl])
-    other = swapped(five, "atom", 0)
+    half = coords.shape[2] // TILE
+    own = jnp.concatenate(
+        [
+            coupling.reshape(2, half, TILE),
+            coords.reshape(3, half, TILE),
+            velocities.reshape(3, half, TILE),
+        ]
+    )
+    pair2 = swapped(own, "lam", 1)
+    pair1 = swapped(own, "lam", 0)
+    other = swapped(own[:5], "atom", 0)
+
     look = lookup(charges, types, type_sigma, type_eps).reshape(3, 2 * half, TILE)
-    first = lax.axis_index("atom") * half
-    tiles = 2 * half
-    local = jnp.mod(near_tiles.reshape(-1) - first + tiles, tiles)
     replica = lax.axis_index("lam")
     cycle = lax.axis_size("lam")
     odd = replica % 2
     flag1 = accept[replica - odd]
     flag2 = accept[jnp.mod(replica - 1 + odd + cycle, cycle)]
-    near = jnp.concatenate([local, jnp.stack([first, flag1, flag2, odd])]).astype(jnp.int32)
-
-    other, look, near = lax.optimization_barrier((other, look, near))
-    ten = jnp.concatenate([cpl, other[3:], pos, moving])
-    pair1 = swapped(ten, "lam", 0)
-    pair2 = swapped(ten, "lam", 1)
-
-    energy, force, new_coords, new_velocities = call_kernel(
-        (near, five, moving, other, pair1, pair2, look), half, listed
+    info = jnp.stack([lax.axis_index("atom") * half, flag1, flag2, odd]).astype(jnp.int32)
+
+    pair1, pair2, other, look, info = lax.optimization_barrier((pair1, pair2, other, look, info))
+    far = swapped(jnp.concatenate([pair1[:2], pair2[:2]]), "atom", 0)
+    energy, force, new_coords, new_velocities = call_kernels(
+        near_tiles, info, own, other, pair1, pair2, far, look
     )
     part = energy[:, :3]
     shape = coords.shape

time: 51.9 us -> 55.8 us (1.075)
  other arithmetic: 0.58 us -> 5.29 us
  local copies, waits for them, and re-layouts: 5.26 us -> 2.3 us
  Pallas kernels: 26.2 us -> 27.7 us
  waiting for transfers between devices: 6.57 us -> 5.57 us
  matrix products: 0.42 us -> 1.27 us
  starting transfers between devices: 11.8 us -> 12.6 us
    unnamed x18 -> x5, local copies, waits for them, and re-layouts: 3.06 us -> 0.96 us
    concatenate x2 -> x3, other arithmetic: 0.03 us -> 1.87 us  [the longest x2 1.86 us: per_device(): jnp.concatenate([coupling.reshape(2, half, TILE), coords.reshape(3, half,...]
    pallas_call x1 -> x2, Pallas kernels: 26.2 us -> 27.7 us  [the longest x1 25.8 us: call_kernels(): pl.pallas_call(partial(tile_kernel, half=half, listed=listed), out_shape=...]
    concatenate x1 -> x0, local copies, waits for them, and re-layouts: 1.37 us -> none  [per_device(): jnp.concatenate([local, jnp.stack([first, flag1, flag2, odd])])]
    another operation x0 -> x1, other arithmetic: none -> 1.37 us  [per_device(): jnp.stack([lax.axis_index('atom') * half, flag1, flag2, odd])]
    ppermute x4 -> x5, waiting for transfers between devices: 6.57 us -> 5.57 us  [swapped(): return lax.ppermute(x, axis, pairs)]
    dot_general x1, matrix products: 0.42 us -> 1.27 us  [lookup(): looked = jnp.dot(table, onehot, precision=lax.Precision.HIGHEST)]
    concatenate x1, other arithmetic: 0.01 us -> 0.86 us  [lookup(): return jnp.concatenate([charges[None], looked])]
  transfers between devices with their start and end apart: 4 -> 5, of which waited for: 2 -> 2; matrix products, arithmetic and copies ran while one was open for 5% -> 12% of each run, Pallas kernels for 0% -> 3%
where the time goes in v4:
time: 55.8 us; the launch traced here: 55.5 us
  Pallas kernels  27.7 us (50%)
  starting transfers between devices  12.6 us (23%)
  waiting for transfers between devices  5.57 us (10%)
  other arithmetic  5.29 us (9%)
  local copies, waits for them, and re-layouts  2.3 us (4%)
  matrix products  1.27 us (2%)
  between operations  0.76 us (1%)
    pallas_call x1, Pallas kernels, call_kernels(): pl.pallas_call(partial(tile_kernel, half=half, listed=listed), out_shape=...  25.8 us
    ppermute x5, starting transfers between devices, swapped(): return lax.ppermute(x, axis, pairs)  12.6 us
    ppermute x5, waiting for transfers between devices, swapped(): return lax.ppermute(x, axis, pairs)  5.57 us
    concatenate x2, other arithmetic, per_device(): jnp.concatenate([coupling.reshape(2, half, TILE), coords.reshape(3, half,...  1.86 us
    pallas_call x1, Pallas kernels, call_kernels(): pl.pallas_call(partial(place_kernel, half=half), out_shape=(jax.ShapeDtyp...  1.82 us
    another operation x1, other arithmetic, per_device(): jnp.stack([lax.axis_index('atom') * half, flag1, flag2, odd])  1.37 us
    dynamic_slice x1, local copies, waits for them, and re-layouts, per_device(): flag1 = accept[replica - odd]  1.32 us
    dot_general x1, matrix products, lookup(): looked = jnp.dot(table, onehot, precision=lax.Precision.HIGHEST)  1.27 us
  transfers between devices with their start and end apart: 5, of which 2 were waited for; matrix products, arithmetic and copies ran while one was open for 12% of the time, Pallas kernels for 3%

profile of v4, /device:TPU:8, one launch (start us, length us, event | category | flops | bytes accessed | tf_op | source)
XLA Modules:
  0.0 55.5 jit_solution(11234386454066465941)
XLA Ops:
  0.6 0.0 copy-start
  0.6 0.9 %copy.26 = f32[1,2,64,128]{3,2,1,0:T(8,128)S(1)} copy(f32[1,2,64,128]{3,1,2,0:T(2,128)} %bitcast.30) | data formatting | bytes 131072
  1.5 1.0 %pad_maximum_fusion.own_ref = f32[8,64,128]{2,1,0:T(8,128)S(1)} fusion(f32[3,64,128]{2,1,0:T(8,128)} %bitcast.29, f32[3,64,128]{2,1,0:T(8,128)} %bitcast.27, f32[2,64,128]{2,1,0:T(8,128)S(1)} %bitcast.24), kind=kLoop, calls=%fused_computation.3 | loop fusion | flops 131072 | bytes 524288 | tf_op jit(solution)/shard_map/concatenate | solution.py:307
  2.5 9.3 %collective-permute-start.1 = (f32[8,64,128]{2,1,0:T(8,128)S(1)}, f32[8,64,128]{2,1,0:T(8,128)S(1)}, u32[]{:S(2)}, u32[]{:S(2)}) collective-permute-start(f32[8,64,128]{2,1,0:T(8,128)S(1)} %pad_maximum_fusion.own_ref), channel_id=1, source_target_pairs={{2,4},{4,2},{6,8},{8,6},{10,12},{12,10},{14,16},{16,14},{18,20},{2... | collective-permute-start | bytes 786440 | tf_op jit(solution)/shard_map/ppermute | solution.py:26
  11.8 0.0 collective-permute-start
  11.8 0.9 %pad_maximum_fusion.2 = f32[5,64,128]{2,1,0:T(8,128)S(1)} fusion(f32[3,64,128]{2,1,0:T(8,128)} %bitcast.28, f32[2,64,128]{2,1,0:T(8,128)S(1)} %bitcast.25), kind=kLoop, calls=%fused_computation.5 | loop fusion | flops 40960 | bytes 327680 | tf_op jit(solution)/shard_map/concatenate | solution.py:307
  12.7 1.4 %collective-permute-start.2 = (f32[5,64,128]{2,1,0:T(8,128)S(1)}, f32[5,64,128]{2,1,0:T(8,128)S(1)}, u32[]{:S(2)}, u32[]{:S(2)}) collective-permute-start(f32[5,64,128]{2,1,0:T(8,128)S(1)} %pad_maximum_fusion.2), channel_id=1, source_target_pairs={{0,1},{1,0},{2,3},{3,2},{4,5},{5,4},{6,7},{7,6},{8,9},{9,8},{10,11... | collective-permute-start | bytes 491528 | tf_op jit(solution)/shard_map/ppermute | solution.py:26
  14.1 0.7 %multiply_bitcast_fusion = (f32[1,16]{1,0:T(1,128)S(1)}, f32[1,16]{1,0:T(1,128)S(1)}) fusion(f32[16]{0:T(128)} %param.14, f32[16]{0:T(128)} %param.15), kind=kLoop, calls=%fused_computation.13 | loop fusion | flops 16 | bytes 256 | tf_op jit(solution)/shard_map/stack | solution.py:255
  14.8 1.3 %convolution_bitcast_fusion = f32[1,2,128,128]{3,1,2,0:T(2,128)S(1)} fusion(s32[16384]{0:T(1024)} %param.13, f32[1,16]{1,0:T(1,128)S(1)} %get-tuple-element.38, f32[1,16]{1,0:T(1,128)S(1)} %get-tuple-element.39), kind=kOutput, calls=%fused_computation | convolution fusion | flops 6553632 | bytes 196736 | tf_op jit(solution)/shard_map/dot_general | solution.py:256
  16.1 1.3 %fusion.5 = (s32[1]{0:T(128)}, s32[1]{0:T(128)}) fusion(s32[128]{0:T(128)} %param.17, s32[]{:T(128)S(6)} %select_n.18, s32[]{:T(128)S(6)} %select_n.20), kind=kLoop, calls=%fused_computation.17 | loop fusion | bytes 24 | tf_op jit(solution)/shard_map/dynamic_slice | solution.py:322
  17.4 1.4 %pad_add_fusion.info_ref = s32[4]{0:T(128)S(1)} fusion(s32[1]{0:T(128)} %bitcast.6, s32[1]{0:T(128)} %get-tuple-element.37, s32[1]{0:T(128)} %get-tuple-element.36, s32[1]{0:T(128)} %bitcast.5), kind=kLoop, calls=%fused_computation.12 | loop fusion | flops 12 | bytes 32 | tf_op jit(solution)/shard_map/stack | solution.py:324
  18.8 0.9 %pad_maximum_fusion.1.look_ref = f32[3,128,128]{2,1,0:T(8,128)S(1)} fusion(f32[2,128,128]{2,1,0:T(8,128)S(1)} %bitcast.26, f32[1,128,128]{2,1,0:T(8,128)} %bitcast.31), kind=kLoop, calls=%fused_computation.4 | loop fusion | flops 49152 | bytes 393216 | tf_op jit(solution)/shard_map/concatenate | solution.py:257
  19.7 0.0 collective-permute-done.2.other_ref
  19.7 0.0 collective-permute-done.1.pair2_ref
  19.7 0.0 collective-permute-done.pair1_ref
  19.7 1.1 %collective-permute-start.3 = (f32[4,64,128]{2,1,0:T(8,128)S(1)}, f32[4,64,128]{2,1,0:T(8,128)S(1)}, u32[]{:S(2)}, u32[]{:S(2)}) collective-permute-start(f32[4,64,128]{2,1,0:T(8,128)S(1)} %pad_maximum_fusion.3), channel_id=1, source_target_pairs={{0,1},{1,0},{2,3},{3,2},{4,5},{5,4},{6,7},{7,6},{8,9},{9,8},{10,11... | collective-permute-start | bytes 393224 | tf_op jit(solution)/shard_map/ppermute | solution.py:26
  20.9 0.0 copy-done
  20.9 0.1 copy.17.near_ref
  21.0 1.8 %places.1 = (bf16[128,48,128]{2,1,0:T(8,128)(2,1)S(1)}, bf16[64,48,384]{2,1,0:T(8,128)(2,1)S(1)}, f32[64,8,128]{2,1,0:T(8,128)S(1)}) custom-call(s32[4]{0:T(128)S(1)} %pad_add_fusion.info_ref, f32[8,64,128]{2,1,0:T(8,128)S(1)} %pad_maximum_fusion.own_ref, f32[5,64,128]{2,1,0:T(8,128)S(1)} %collective-permute-done.2.other_ref, ...), custom_call_target="tpu_custom_call" | custom-call | tf_op jit(solution)/shard_map/places/pallas_call | solution.py:267
  22.8 2.7 %collective-permute-done.3.far_ref = f32[4,64,128]{2,1,0:T(8,128)S(1)} collective-permute-done((f32[4,64,128]{2,1,0:T(8,128)S(1)}, f32[4,64,128]{2,1,0:T(8,128)S(1)}, u32[]{:S(2)}, u32[]{:S(2)}) %collective-permute-start.3) | collective-permute-done | bytes 131104 | tf_op jit(solution)/shard_map/ppermute | solution.py:26
  25.5 25.8 %tiles.1 = (f32[1,128]{1,0:T(1,128)S(1)}, f32[3,64,128]{2,1,0:T(8,128)}, f32[3,64,128]{2,1,0:T(8,128)}, f32[3,64,128]{2,1,0:T(8,128)}) custom-call(s32[64,5]{1,0:T(8,128)S(1)} %copy.17.near_ref, s32[4]{0:T(128)S(1)} %pad_add_fusion.info_ref, f32[8,64,128]{2,1,0:T(8,128)S(1)} %pad_maximum_fusion.own_ref, f32[5,64,128]{2,1,0:T(8,128)S(1)} %collective-permute-done.2.other_ref, ...), custom_call_target="tpu_custom_call" | custom-call | tf_op jit(solution)/shard_map/tiles/pallas_call | solution.py:279
  51.3 0.8 %collective-permute-start.4 = (f32[1,3]{1,0:T(1,128)S(1)}, f32[1,3]{1,0:T(1,128)S(1)}, u32[]{:S(2)}, u32[]{:S(2)}) collective-permute-start(f32[1,3]{1,0:T(1,128)S(1)} %bitcast.23), channel_id=1, source_target_pairs={{0,1},{1,0},{2,3},{3,2},{4,5},{5,4},{6,7},{7,6},{8,9},{9,8},{10,11... | collective-permute-start | bytes 44 | tf_op jit(solution)/shard_map/ppermute | solution.py:26
  52.1 2.9 %collective-permute-done.4 = f32[1,3]{1,0:T(1,128)S(1)} collective-permute-done((f32[1,3]{1,0:T(1,128)S(1)}, f32[1,3]{1,0:T(1,128)S(1)}, u32[]{:S(2)}, u32[]{:S(2)}) %collective-permute-start.4) | collective-permute-done | bytes 44 | tf_op jit(solution)/shard_map/ppermute | solution.py:26
  55.0 0.5 slice_add_fusion
  (4 shorter events, 0.0 us)
Async XLA Ops:
  0.6 20.2 %copy-start = (s32[64,5]{0,1:T(8,128)S(1)}, s32[64,5]{0,1:T(8,128)}, u32[]{:S(2)}) copy-start(s32[64,5]{0,1:T(8,128)} %param.16) | copy-start | bytes 3844
  2.5 17.2 %collective-permute-start.1 = (f32[8,64,128]{2,1,0:T(8,128)S(1)}, f32[8,64,128]{2,1,0:T(8,128)S(1)}, u32[]{:S(2)}, u32[]{:S(2)}) collective-permute-start(f32[8,64,128]{2,1,0:T(8,128)S(1)} %pad_maximum_fusion.own_ref), channel_id=1, source_target_pairs={{2,4},{4,2},{6,8},{8,6},{10,12},{12,10},{14,16},{16,14},{18,20},{2... | collective-permute-start | bytes 786440 | tf_op jit(solution)/shard_map/ppermute | solution.py:26
  11.8 7.9 %collective-permute-start = (f32[8,64,128]{2,1,0:T(8,128)S(1)}, f32[8,64,128]{2,1,0:T(8,128)S(1)}, u32[]{:S(2)}, u32[]{:S(2)}) collective-permute-start(f32[8,64,128]{2,1,0:T(8,128)S(1)} %pad_maximum_fusion.own_ref), channel_id=1, source_target_pairs={{0,2},{2,0},{4,6},{6,4},{8,10},{10,8},{12,14},{14,12},{16,18},{18,... | collective-permute-start | bytes 786440 | tf_op jit(solution)/shard_map/ppermute | solution.py:26
  12.7 7.0 %collective-permute-start.2 = (f32[5,64,128]{2,1,0:T(8,128)S(1)}, f32[5,64,128]{2,1,0:T(8,128)S(1)}, u32[]{:S(2)}, u32[]{:S(2)}) collective-permute-start(f32[5,64,128]{2,1,0:T(8,128)S(1)} %pad_maximum_fusion.2), channel_id=1, source_target_pairs={{0,1},{1,0},{2,3},{3,2},{4,5},{5,4},{6,7},{7,6},{8,9},{9,8},{10,11... | collective-permute-start | bytes 491528 | tf_op jit(solution)/shard_map/ppermute | solution.py:26
  19.7 5.7 %collective-permute-start.3 = (f32[4,64,128]{2,1,0:T(8,128)S(1)}, f32[4,64,128]{2,1,0:T(8,128)S(1)}, u32[]{:S(2)}, u32[]{:S(2)}) collective-permute-start(f32[4,64,128]{2,1,0:T(8,128)S(1)} %pad_maximum_fusion.3), channel_id=1, source_target_pairs={{0,1},{1,0},{2,3},{3,2},{4,5},{5,4},{6,7},{7,6},{8,9},{9,8},{10,11... | collective-permute-start | bytes 393224 | tf_op jit(solution)/shard_map/ppermute | solution.py:26
  51.3 3.7 %collective-permute-start.4 = (f32[1,3]{1,0:T(1,128)S(1)}, f32[1,3]{1,0:T(1,128)S(1)}, u32[]{:S(2)}, u32[]{:S(2)}) collective-permute-start(f32[1,3]{1,0:T(1,128)S(1)} %bitcast.23), channel_id=1, source_target_pairs={{0,1},{1,0},{2,3},{3,2},{4,5},{5,4},{6,7},{7,6},{8,9},{9,8},{10,11... | collective-permute-start | bytes 44 | tf_op jit(solution)/shard_map/ppermute | solution.py:26
